TPU v7x, 32 devices: a whole 2x2x4 slice. The times are simulated.
32 devices in a mesh: grp: 2 (over y), wide: 8 (over z, x), narrow: 2 (over core).
Axes of the slice: x: 2, y: 2, z: 4, core: 2. Of those that a mesh axis runs over, the one named last changes fastest.
Arguments:
- denoised: float32 [4, 512, 512], P('grp', 'wide', 'narrow'), parts along dimension 0, may hold values from -6 to 6
- clean_volume: float32 [4, 512, 512], P('grp', 'wide', 'narrow'), parts along dimension 0, may hold values from -6 to 6
- weight: float32 [512, 512], P(('wide', 'narrow')), may hold values from 0.1 to 2
- act_in: bfloat16 [64, 4, 512, 512], P(None, 'grp', 'wide', 'narrow'), parts along dimension 1, may hold values from -6 to 6
- act_mid: bfloat16 [64, 4, 512, 512], P(None, 'grp', 'wide', 'narrow'), parts along dimension 1, as said below
- w_first: bfloat16 [27, 64, 64], replicated, may hold values from -0.15625 to 0.15625
- w_second: bfloat16 [27, 64], replicated, may hold values from -0.15625 to 0.15625
Outputs:
- grad_in: bfloat16 [64, 4, 512, 512], P(None, 'grp', 'wide', 'narrow'), parts along dimension 1
- grad_first: float32 [54, 64, 64], P('grp'), parts along dimension 0
- grad_second: float32 [54, 64], P('grp'), parts along dimension 0
There are 2 independent parts, one for each index of `grp`. A program takes and returns all parts, laid end to end along the dimension named above; an argument that names none is the same for every part. Nothing has to cross between parts.
Inputs may be any that keep to these rules, and one draw needn't show every extreme that they name: act_mid is a rectifier's output: non-negative, with many zeros.
All inputs are finite; a program needn't handle non-finite values.
Results may differ from a plain program's by a relative error of at most 0.0058.
Values may be sent and summed in bfloat16 or wider, within the bound.
No kernel may reach another device: no remote copies, remote signals or barrier semaphores. Data moves between devices by JAX's collectives and lax.ppermute only.
A program may use at most 320 MiB of HBM per device.

v0:
```python
import jax
import jax.numpy as jnp
from jax import lax
from jax.sharding import PartitionSpec as P

two_pi = 6.283185307179586
highest = lax.Precision.HIGHEST


def with_halo(x, sides, width):
    for axis, dim in sides:
        devices, length = (lax.axis_size(axis), x.shape[dim])
        up = [(i, (i + 1) % devices) for i in range(devices - 1)]
        down = [(j, i) for i, j in up]
        last = lax.slice_in_dim(x, length - width, length, axis=dim)
        first = lax.slice_in_dim(x, 0, width, axis=dim)
        before = lax.ppermute(last, axis, up)
        after = lax.ppermute(first, axis, down)
        x = jnp.concatenate([before, x, after], axis=dim)
    return x


def phase_table(left_index, right_index, length):
    product = left_index[:, None] * right_index[None, :] % length
    angles = product.astype(jnp.float32) * (two_pi / length)
    return (jnp.cos(angles), jnp.sin(angles))


def shifted_windows(padded, slices, rows_x, cols_y, taps_list):
    windows = []
    for tap_index in taps_list:
        step_z = tap_index // 9 - 1
        step_x = tap_index // 3 % 3 - 1
        step_y = tap_index % 3 - 1
        windows.append(
            padded[
                ...,
                1 - step_z : 1 - step_z + slices,
                1 - step_x : 1 - step_x + rows_x,
                1 - step_y : 1 - step_y + cols_y,
            ]
        )
    return jnp.stack(windows, axis=0)


def shards(denoised, clean_volume, weight, act_in, act_mid, w_first, w_second):
    wide_count = lax.axis_size("wide")
    narrow_count = lax.axis_size("narrow")
    slices, rows_x, half_cols = denoised.shape
    total_y = half_cols * narrow_count
    total_x = rows_x * wide_count
    kept_cols = half_cols // wide_count
    narrow_index = lax.axis_index("narrow")
    error_field = denoised - clean_volume
    columns = lax.iota(jnp.int32, total_y)
    frequency = (
        columns % half_cols // kept_cols * narrow_count + columns // half_cols
    ) * kept_cols + columns % kept_cols
    own_rows = narrow_index * half_cols + lax.iota(jnp.int32, half_cols)
    cos_y, sin_y = phase_table(own_rows, frequency, total_y)
    part_real = jnp.einsum("zxy,yc->zxc", error_field, cos_y, precision=highest)
    part_imag = -jnp.einsum("zxy,yc->zxc", error_field, sin_y, precision=highest)
    spec_real, spec_imag = (
        lax.psum_scatter(part_real, "narrow", scatter_dimension=2, tiled=True),
        lax.psum_scatter(part_imag, "narrow", scatter_dimension=2, tiled=True),
    )
    positions = lax.iota(jnp.int32, total_x)
    cos_x, sin_x = phase_table(positions, positions, total_x)
    pieces = (
        lax.all_to_all(
            spec_real.reshape(slices, rows_x, wide_count, kept_cols),
            "wide",
            split_axis=2,
            concat_axis=1,
            tiled=True,
        ),
        lax.all_to_all(
            spec_imag.reshape(slices, rows_x, wide_count, kept_cols),
            "wide",
            split_axis=2,
            concat_axis=1,
            tiled=True,
        ),
    )
    item_count = pieces[0].shape[0]
    in_real = pieces[0].reshape(item_count, total_x, kept_cols)
    in_imag = pieces[1].reshape(item_count, total_x, kept_cols)
    four_real = jnp.einsum("mxk,xq->mkq", in_real, cos_x, precision=highest) + jnp.einsum(
        "mxk,xq->mkq", in_imag, sin_x, precision=highest
    )
    four_imag = jnp.einsum("mxk,xq->mkq", in_imag, cos_x, precision=highest) - jnp.einsum(
        "mxk,xq->mkq", in_real, sin_x, precision=highest
    )
    weighted_real = weight * four_real
    weighted_imag = weight * four_imag
    out_real = jnp.einsum("mkq,qx->mxk", weighted_real, cos_x, precision=highest) - jnp.einsum(
        "mkq,qx->mxk", weighted_imag, sin_x, precision=highest
    )
    out_imag = jnp.einsum("mkq,qx->mxk", weighted_imag, cos_x, precision=highest) + jnp.einsum(
        "mkq,qx->mxk", weighted_real, sin_x, precision=highest
    )
    back_real = lax.all_to_all(
        out_real.reshape(item_count, wide_count, rows_x, kept_cols),
        "wide",
        split_axis=1,
        concat_axis=3,
        tiled=True,
    ).reshape(item_count, rows_x, half_cols)
    back_imag = lax.all_to_all(
        out_imag.reshape(item_count, wide_count, rows_x, kept_cols),
        "wide",
        split_axis=1,
        concat_axis=3,
        tiled=True,
    ).reshape(item_count, rows_x, half_cols)
    local_cols = lax.iota(jnp.int32, half_cols)
    own_freq = (
        local_cols // kept_cols * narrow_count + narrow_index
    ) * kept_cols + local_cols % kept_cols
    cos_back, sin_back = phase_table(own_freq, columns, total_y)
    part_term = jnp.einsum("zxc,cy->zxy", back_real, cos_back, precision=highest) - jnp.einsum(
        "zxc,cy->zxy", back_imag, sin_back, precision=highest
    )
    field_real = lax.psum_scatter(part_term, "narrow", scatter_dimension=2, tiled=True)
    grad_noise = (field_real * (-2.0 / (total_x * total_y))).astype(jnp.bfloat16)
    noise_rim = with_halo(grad_noise, (("wide", 1), ("narrow", 2)), 1)
    noise_pad = jnp.pad(noise_rim, ((1, 1), (0, 0), (0, 0)))
    noise_windows = shifted_windows(noise_pad, slices, rows_x, half_cols, range(27))
    grad_mid = jnp.einsum(
        "tc,tzxy->czxy", w_second, noise_windows, preferred_element_type=jnp.float32
    )
    masked = jnp.where(act_mid > 0, grad_mid, 0.0).astype(jnp.bfloat16)
    masked_rim = with_halo(masked, (("wide", 2), ("narrow", 3)), 1)
    grad_second = jnp.einsum(
        "czxy,tzxy->tc", act_mid, noise_windows, preferred_element_type=jnp.float32
    )
    masked_pad = jnp.pad(masked_rim, ((0, 0), (1, 1), (0, 0), (0, 0)))
    channels = act_in.shape[0]
    grad_in = jnp.zeros(act_in.shape, jnp.float32)
    first_parts = []
    for plane_index in range(9):
        stacked = shifted_windows(
            masked_pad, slices, rows_x, half_cols, [plane_index, plane_index + 9, plane_index + 18]
        )
        first_parts.append(
            jnp.einsum("izxy,dozxy->dio", act_in, stacked, preferred_element_type=jnp.float32)
        )
        grad_in = grad_in + jnp.einsum(
            "dio,dozxy->izxy", w_first[plane_index::9], stacked, preferred_element_type=jnp.float32
        )
    grad_first = jnp.stack(first_parts, axis=1).reshape(27, channels, channels)
    grad_first, grad_second = lax.psum((grad_first, grad_second), ("wide", "narrow"))
    return (grad_in.astype(jnp.bfloat16), grad_first, grad_second)


def solution(mesh):
    placed = (
        P("grp", "wide", "narrow"),
        P("grp", "wide", "narrow"),
        P(("wide", "narrow"), None),
        P(None, "grp", "wide", "narrow"),
        P(None, "grp", "wide", "narrow"),
        P(),
        P(),
    )
    return jax.shard_map(
        shards,
        mesh=mesh,
        in_specs=placed,
        out_specs=(P(None, "grp", "wide", "narrow"), P("grp", None, None), P("grp", None)),
        check_vma=False,
    )
```

profile of v0, /device:TPU:0, one launch (start us, length us, event | category | flops | bytes accessed | tf_op | source)
XLA Modules:
  0.0 590.2 jit_solution(6544291308981167660)
XLA Ops:
  15.5 6.4 %reduce-scatter.4.cloned.1.call-done = f32[2,64,256]{2,1,0:T(8,128)} async-done(((f32[2,64,512]{2,1,0:T(8,128)}), f32[2,64,256]{2,1,0:T(8,128)}) %reduce-scatter.4.cloned.1.call-update) | async-done | bytes 131088 | tf_op jit(solution)/shard_map/reduce_scatter | solution.py:64
  23.8 5.7 all-to-all-start
  98.9 6.0 %all-to-all-done.3 = f32[8,1,4096]{2,1,0:T(1,128)S(1)} async-done(((f32[8,1,4096]{2,1,0:T(1,128)}), f32[8,1,4096]{2,1,0:T(1,128)S(1)}, u32[]{:S(2)}, u32[]{:S(2)}) %all-to-all-start.3) | async-done | bytes 131104 | tf_op jit(solution)/shard_map/all_to_all | solution.py:109
  147.6 6.3 %fusion.100 = f32[27,64]{1,0:T(8,128)S(1)} fusion(bf16[64,2,64,256]{3,2,1,0:T(8,128)(2,1)S(1)} %copy-done.27, bf16[27,2,64,256]{3,2,1,0:T(8,128)(2,1)S(1)} %constant_dynamic-update-slice_fusion), kind=kOutput, calls=%fused_computation.124 | convolution fusion | flops 113246208 | bytes 5970688 | tf_op jit(solution)/shard_map/czxy,tzxy->tc/dot_general | solution.py:134
  154.0 60.0 %psum.15 = f32[27,64]{1,0:T(8,128)} all-reduce(f32[27,64]{1,0:T(8,128)S(1)} %fusion.100), channel_id=1, replica_groups=mesh['grp'=2,'wide'=8,'narrow'=2] {'wide','narrow'}, use_global_device_ids=true, to_apply=%region_4.5 | all-reduce | flops 1728 | bytes 13824 | tf_op jit(solution)/shard_map/psum | solution.py:152
  227.9 5.8 fusion.27
  242.7 8.2 %pad_maximum_fusion.9 = (bf16[64,2,66,257]{3,0,2,1:T(8,128)(2,1)S(1)}, bf16[64,2,66,257]{3,0,2,1:T(8,128)(2,1)S(1)}) fusion(bf16[64,2,66,1]{3,0,2,1:T(8,128)(2,1)} %copy.104, bf16[64,2,1,256]{3,0,2,1:T(8,128)(2,1)S(1)} %collective-permute-done.5, bf16[64,2,64,256]{3,0,2,1:T(8,128)(2,1)} %copy-done.2, bf16[64,2,1,256]{3,0,2,1:T(8,128)(2,1)S(1)} %collective-permute-done.4, ...), kind=kLoop, calls=%fused_computation.30 | loop fusion | flops 34738176 | bytes 13043712 | tf_op jit(solution)/shard_map/concatenate | solution.py:19
  250.9 9.2 %slice_bitcast_fusion.22 = (bf16[1,64,2,64,256]{4,1,3,2,0:T(8,128)(2,1)}, bf16[1,64,2,64,256]{4,1,3,2,0:T(8,128)(2,1)}, bf16[1,64,2,64,256]{4,1,3,2,0:T(8,128)(2,1)}) fusion(bf16[64,2,66,257]{3,0,2,1:T(8,128)(2,1)S(1)} %get-tuple-element.36), kind=kLoop, calls=%fused_computation.77 | loop fusion | bytes 25165824 | tf_op jit(solution)/shard_map/stack | solution.py:43
  260.1 8.9 %select_maximum_fusion = bf16[64,4,66,258]{3,0,2,1:T(8,128)(2,1)} fusion(bf16[64,2,66,1]{3,0,2,1:T(8,128)(2,1)} %copy.104, bf16[64,2,66,1]{3,0,2,1:T(8,128)(2,1)S(1)} %copy-done.4, bf16[64,2,1,256]{3,0,2,1:T(8,128)(2,1)S(1)} %collective-permute-done.5, bf16[64,2,64,256]{3,0,2,1:T(8,128)(2,1)S(1)} %copy-done.3, ...), kind=kLoop, calls=%fused_computation.3 | loop fusion | flops 78465024 | bytes 13077504 | tf_op jit(solution)/shard_map/concatenate | solution.py:19
  269.1 64.1 %slice_bitcast_fusion.23 = (bf16[1,64,2,64,256]{4,1,3,2,0:T(8,128)(2,1)}, bf16[1,64,2,64,256]{4,1,3,2,0:T(8,128)(2,1)}, bf16[1,64,2,64,256]{4,1,3,2,0:T(8,128)(2...) fusion(bf16[64,4,66,258]{3,0,2,1:T(8,128)(2,1)} %select_maximum, ...), kind=kLoop, calls=%fused_computation.78 | loop fusion | bytes 150994944 | tf_op jit(solution)/shard_map/stack | solution.py:43
  333.2 15.3 %fusion.49 = f32[3,9,64,64]{2,3,0,1:T(8,128)} fusion(bf16[1,64,2,64,256]{4,1,3,2,0:T(8,128)(2,1)} %get-tuple-element.28, bf16[1,64,2,64,256]{4,1,3,2,0:T(8,128)(2,1)} %get-tuple-element.30, bf16[1,64,2,64,256]{4,1,3,2,0:T(8,128)(2,1)} %get-tuple-element.12, bf16[64,2,64,256,1]{3,2,1,0,4:T(8,128)(2,1)} %bitcast.559), kind=kOutput, calls=%fused_computation.107 | convolution fusion | flops 817889280 | bytes 16875520 | tf_op jit(solution)/shard_map/izxy,dozxy->dio/dot_general | solution.py:146
  348.6 8.5 %fusion.25 = f32[2,64,256,64,1]{2,3,1,0,4:T(8,128)} fusion(bf16[1,64,2,64,256]{4,1,3,2,0:T(8,128)(2,1)} %get-tuple-element.28, bf16[1,64,2,64,256]{4,1,3,2,0:T(8,128)(2,1)} %get-tuple-element.30, bf16[1,64,2,64,256]{4,1,3,2,0:T(8,128)(2,1)} %get-tuple-element.12, bf16[27,64,64]{2,1,0:T(8,128)(2,1)S(1)} %copy-done.29), kind=kOutput, calls=%fused_computation.49 | convolution fusion | flops 843055104 | bytes 21020672 | tf_op jit(solution)/shard_map/dio,dozxy->izxy/dot_general | solution.py:148
  365.0 9.2 %fusion.55 = f32[3,9,64,64]{2,3,0,1:T(8,128)} fusion(f32[3,9,64,64]{2,3,0,1:T(8,128)} %fusion.49, bf16[1,64,2,64,256]{4,1,3,2,0:T(8,128)(2,1)S(1)} %copy-done.21, bf16[1,64,2,64,256]{4,1,3,2,0:T(8,128)(2,1)S(1)} %copy-done.10, bf16[1,64,2,64,256]{4,1,3,2,0:T(8,128)(2,1)S(1)} %copy-done.22, bf16[64,2,64,256,1]{3,2,1,0,4:T(8,128)(2,1)} %bitcast.560), kind=kOutput, calls=%fused_computation.109 | convolution fusion | flops 817889280 | bytes 16875520 | tf_op jit(solution)/shard_map/izxy,dozxy->dio/dot_general | solution.py:146
  387.2 10.4 %fusion.61 = f32[3,9,64,64]{2,3,0,1:T(8,128)} fusion(f32[3,9,64,64]{2,3,0,1:T(8,128)} %fusion.55, bf16[1,64,2,64,256]{4,1,3,2,0:T(8,128)(2,1)S(1)} %copy-done.19, bf16[1,64,2,64,256]{4,1,3,2,0:T(8,128)(2,1)} %copy-done.26, bf16[1,64,2,64,256]{4,1,3,2,0:T(8,128)(2,1)S(1)} %copy-done.20, bf16[64,2,64,256,1]{3,2,1,0,4:T(8,128)(2,1)} %bitcast.561), kind=kOutput, calls=%fused_computation.111 | convolution fusion | flops 817889280 | bytes 16875520 | tf_op jit(solution)/shard_map/izxy,dozxy->dio/dot_general | solution.py:146
  397.6 6.5 %fusion.19 = f32[2,64,256,64,1]{2,3,1,0,4:T(8,128)} fusion(bf16[1,64,2,64,256]{4,1,3,2,0:T(8,128)(2,1)S(1)} %copy-done.17, bf16[1,64,2,64,256]{4,1,3,2,0:T(8,128)(2,1)} %get-tuple-element.32, bf16[1,64,2,64,256]{4,1,3,2,0:T(8,128)(2,1)S(1)} %copy-done.18, bf16[27,64,64]{2,1,0:T(8,128)(2,1)S(1)} %copy-done.29), kind=kOutput, calls=%fused_computation.43 | convolution fusion | flops 843055104 | bytes 21020672 | tf_op jit(solution)/shard_map/dio,dozxy->izxy/dot_general | solution.py:148
  404.2 10.4 %fusion.67 = f32[3,9,64,64]{2,3,0,1:T(8,128)} fusion(f32[3,9,64,64]{2,3,0,1:T(8,128)} %fusion.61, bf16[1,64,2,64,256]{4,1,3,2,0:T(8,128)(2,1)S(1)} %copy-done.17, bf16[1,64,2,64,256]{4,1,3,2,0:T(8,128)(2,1)} %get-tuple-element.32, bf16[1,64,2,64,256]{4,1,3,2,0:T(8,128)(2,1)S(1)} %copy-done.18, bf16[64,2,64,256,1]{3,2,1,0,4:T(8,128)(2,1)} %bitcast.562), kind=kOutput, calls=%fused_computation.113 | convolution fusion | flops 817889280 | bytes 16875520 | tf_op jit(solution)/shard_map/izxy,dozxy->dio/dot_general | solution.py:146
  420.0 9.3 %fusion.73 = f32[3,9,64,64]{2,3,0,1:T(8,128)} fusion(f32[3,9,64,64]{2,3,0,1:T(8,128)} %fusion.67, bf16[1,64,2,64,256]{4,1,3,2,0:T(8,128)(2,1)S(1)} %copy-done.15, bf16[1,64,2,64,256]{4,1,3,2,0:T(8,128)(2,1)S(1)} %bitcast.549, bf16[1,64,2,64,256]{4,1,3,2,0:T(8,128)(2,1)S(1)} %copy-done.16, bf16[64,2,64,256,1]{3,2,1,0,4:T(8,128)(2,1)} %bitcast.563), kind=kOutput, calls=%fused_computation.115 | convolution fusion | flops 817889280 | bytes 16875520 | tf_op jit(solution)/shard_map/izxy,dozxy->dio/dot_general | solution.py:146
  429.3 6.6 %fusion.15 = f32[2,64,256,64,1]{2,3,1,0,4:T(8,128)} fusion(bf16[1,64,2,64,256]{4,1,3,2,0:T(8,128)(2,1)S(1)} %copy-done.13, bf16[1,64,2,64,256]{4,1,3,2,0:T(8,128)(2,1)} %get-tuple-element.35, bf16[1,64,2,64,256]{4,1,3,2,0:T(8,128)(2,1)S(1)} %copy-done.14, bf16[27,64,64]{2,1,0:T(8,128)(2,1)S(1)} %copy-done.29), kind=kOutput, calls=%fused_computation.39 | convolution fusion | flops 843055104 | bytes 21020672 | tf_op jit(solution)/shard_map/dio,dozxy->izxy/dot_general | solution.py:148
  436.0 10.4 %fusion.79 = f32[3,9,64,64]{2,3,0,1:T(8,128)} fusion(f32[3,9,64,64]{2,3,0,1:T(8,128)} %fusion.73, bf16[1,64,2,64,256]{4,1,3,2,0:T(8,128)(2,1)S(1)} %copy-done.13, bf16[1,64,2,64,256]{4,1,3,2,0:T(8,128)(2,1)} %get-tuple-element.35, bf16[1,64,2,64,256]{4,1,3,2,0:T(8,128)(2,1)S(1)} %copy-done.14, bf16[64,2,64,256,1]{3,2,1,0,4:T(8,128)(2,1)} %bitcast.564), kind=kOutput, calls=%fused_computation.117 | convolution fusion | flops 817889280 | bytes 16875520 | tf_op jit(solution)/shard_map/izxy,dozxy->dio/dot_general | solution.py:146
  451.8 9.3 %fusion.85 = f32[3,9,64,64]{2,3,0,1:T(8,128)} fusion(f32[3,9,64,64]{2,3,0,1:T(8,128)} %fusion.79, bf16[1,64,2,64,256]{4,1,3,2,0:T(8,128)(2,1)S(1)} %copy-done.11, bf16[1,64,2,64,256]{4,1,3,2,0:T(8,128)(2,1)S(1)} %copy-done.24, bf16[1,64,2,64,256]{4,1,3,2,0:T(8,128)(2,1)S(1)} %copy-done.12, bf16[64,2,64,256,1]{3,2,1,0,4:T(8,128)(2,1)} %bitcast.565), kind=kOutput, calls=%fused_computation.119 | convolution fusion | flops 817889280 | bytes 16875520 | tf_op jit(solution)/shard_map/izxy,dozxy->dio/dot_general | solution.py:146
  466.7 9.3 %fusion.91 = f32[3,9,64,64]{2,3,0,1:T(8,128)} fusion(f32[3,9,64,64]{2,3,0,1:T(8,128)} %fusion.85, bf16[1,64,2,64,256]{4,1,3,2,0:T(8,128)(2,1)S(1)} %copy-done.8, bf16[1,64,2,64,256]{4,1,3,2,0:T(8,128)(2,1)S(1)} %copy-done.5, bf16[1,64,2,64,256]{4,1,3,2,0:T(8,128)(2,1)S(1)} %copy-done.9, bf16[64,2,64,256,1]{3,2,1,0,4:T(8,128)(2,1)} %bitcast.566), kind=kOutput, calls=%fused_computation.121 | convolution fusion | flops 817889280 | bytes 16875520 | tf_op jit(solution)/shard_map/izxy,dozxy->dio/dot_general | solution.py:146
  481.3 6.4 %fusion.97 = f32[3,9,64,64]{2,3,0,1:T(8,128)} fusion(f32[3,9,64,64]{2,3,0,1:T(8,128)} %fusion.91, bf16[1,64,2,64,256]{4,1,3,2,0:T(8,128)(2,1)S(1)} %copy-done.7, bf16[1,64,2,64,256]{4,1,3,2,0:T(8,128)(2,1)S(1)} %copy-done.25, bf16[1,64,2,64,256]{4,1,3,2,0:T(8,128)(2,1)S(1)} %copy-done.6, bf16[64,2,64,256,1]{3,2,1,0,4:T(8,128)(2,1)S(1)} %bitcast.567), kind=kOutput, calls=%fused_computation.123 | convolution fusion | flops 817889280 | bytes 16875520 | tf_op jit(solution)/shard_map/izxy,dozxy->dio/dot_general | solution.py:146
  490.1 25.0 %fusion.39 = bf16[64,2,64,256]{3,0,1,2:T(8,128)(2,1)S(1)} fusion(f32[2,64,256,64,1]{2,3,1,0,4:T(8,128)} %fusion.9, f32[2,64,256,64,1]{2,3,1,0,4:T(8,128)} %fusion.11, f32[2,64,256,64,1]{2,3,1,0,4:T(8,128)} %fusion.13, f32[2,64,256,64,1]{2,3,1,0,4:T(8,128)} %fusion.15, f32[2,64,256,64,1]{2,3,1,0,4:T(8,128)} %fusion.17, f32[2,64,256,64,1]{2,3,1,0,4:T(8,128)} %fusion.19, ...), kind=kLoop, calls=%fused_computation.90 | loop fusion | flops 18874368 | bytes 79691776 | tf_op jit(solution)/shard_map/convert_element_type | solution.py:153
  519.6 61.7 %all-reduce.4.cloned.1.call-done = f32[27,64,64]{2,1,0:T(8,128)} async-done(((f32[27,64,64]{2,1,0:T(8,128)}), f32[27,64,64]{2,1,0:T(8,128)}) %all-reduce.4.cloned.1.call-update) | async-done | bytes 442384 | tf_op jit(solution)/shard_map/psum | solution.py:152
  (191 shorter events, 196.1 us)
Async XLA Ops:
  7.2 128.0 %copy-start = (bf16[27,64]{1,0:T(8,128)(2,1)S(1)}, bf16[27,64]{1,0:T(8,128)(2,1)}, u32[]{:S(2)}) copy-start(bf16[27,64]{1,0:T(8,128)(2,1)} %param.13) | copy-start | bytes 10372
  7.2 14.7 %reduce-scatter.4.cloned.1.call-start = ((), (), s32[]{:S(2)}) async-start(), calls=%async_computation.7 | async-start | bytes 393216 | tf_op jit(solution)/shard_map/reduce_scatter | solution.py:64
  11.4 22.3 %reduce-scatter.6.cloned.1.call-start = ((), (), s32[]{:S(2)}) async-start(), calls=%async_computation.8 | async-start | bytes 393216 | tf_op jit(solution)/shard_map/reduce_scatter | solution.py:65
  23.8 13.2 %all-to-all-start = ((f32[8,1,4096]{2,1,0:T(1,128)}), f32[8,1,4096]{2,1,0:T(1,128)S(1)}, u32[]{:S(2)}, u32[]{:S(2)}) async-start(f32[8,1,4096]{2,1,0:T(1,128)} %reshape.165), calls=%async_computation.1 | async-start | bytes 262144 | tf_op jit(solution)/shard_map/all_to_all | solution.py:70
  37.0 12.2 %all-to-all-start.1 = ((f32[8,1,4096]{2,1,0:T(1,128)}), f32[8,1,4096]{2,1,0:T(1,128)S(1)}, u32[]{:S(2)}, u32[]{:S(2)}) async-start(f32[8,1,4096]{2,1,0:T(1,128)} %reshape.167), calls=%async_computation.3 | async-start | bytes 262144 | tf_op jit(solution)/shard_map/all_to_all | solution.py:77
  80.5 12.6 %all-to-all-start.2 = ((f32[8,1,4096]{2,1,0:T(1,128)}), f32[8,1,4096]{2,1,0:T(1,128)S(1)}, u32[]{:S(2)}, u32[]{:S(2)}) async-start(f32[8,1,4096]{2,1,0:T(1,128)} %reshape.169), calls=%async_computation.4 | async-start | bytes 262144 | tf_op jit(solution)/shard_map/all_to_all | solution.py:102
  93.1 11.8 %all-to-all-start.3 = ((f32[8,1,4096]{2,1,0:T(1,128)}), f32[8,1,4096]{2,1,0:T(1,128)S(1)}, u32[]{:S(2)}, u32[]{:S(2)}) async-start(f32[8,1,4096]{2,1,0:T(1,128)} %reshape.171), calls=%async_computation.5 | async-start | bytes 262144 | tf_op jit(solution)/shard_map/all_to_all | solution.py:109
  97.5 19.8 %reduce-scatter.8.cloned.1.call-start = ((), (), s32[]{:S(2)}) async-start(), calls=%async_computation.9 | async-start | bytes 393216 | tf_op jit(solution)/shard_map/reduce_scatter | solution.py:124
  111.7 469.5 %all-reduce.4.cloned.1.call-start = ((), (), s32[]{:S(2)}) async-start(), calls=%async_computation.10 | async-start | bytes 1769472 | tf_op jit(solution)/shard_map/psum | solution.py:152
  117.3 17.8 %copy-start.27 = (bf16[64,2,64,256]{3,2,1,0:T(8,128)(2,1)S(1)}, bf16[64,2,64,256]{3,2,1,0:T(8,128)(2,1)}, u32[]{:S(2)}) copy-start(bf16[64,2,64,256]{3,2,1,0:T(8,128)(2,1)} %param.11) | copy-start | bytes 12582916
  118.4 5.1 collective-permute-start
  122.2 5.5 collective-permute-start.1
  127.8 2.6 collective-permute-start.2
  129.1 3.1 collective-permute-start.3
  141.7 72.4 %collective-permute-start.4 = (bf16[64,2,1,256]{3,0,2,1:T(8,128)(2,1)S(1)}, bf16[64,2,1,256]{3,0,2,1:T(8,128)(2,1)S(1)}, u32[]{:S(2)}, u32[]{:S(2)}) collective-permute-start(bf16[64,2,1,256]{3,0,2,1:T(8,128)(2,1)S(1)} %get-tuple-element.42), channel_id=1, source_target_pairs={{0,2},{2,4},{4,6},{6,8},{8,10},{10,12},{12,14},{1,3},{3,5},{5,7},{... | collective-permute-start | bytes 196616 | tf_op jit(solution)/shard_map/ppermute | solution.py:17
  145.9 68.1 %collective-permute-start.5 = (bf16[64,2,1,256]{3,0,2,1:T(8,128)(2,1)S(1)}, bf16[64,2,1,256]{3,0,2,1:T(8,128)(2,1)S(1)}, u32[]{:S(2)}, u32[]{:S(2)}) collective-permute-start(bf16[64,2,1,256]{3,0,2,1:T(8,128)(2,1)S(1)} %get-tuple-element.43), channel_id=1, source_target_pairs={{2,0},{4,2},{6,4},{8,6},{10,8},{12,10},{14,12},{3,1},{5,3},{7,5},{... | collective-permute-start | bytes 196616 | tf_op jit(solution)/shard_map/ppermute | solution.py:18
  222.6 11.1 %collective-permute-start.6 = (bf16[64,2,66,1]{2,0,3,1:T(8,128)(2,1)S(1)}, bf16[64,2,66,1]{2,0,3,1:T(8,128)(2,1)S(1)}, u32[]{:S(2)}, u32[]{:S(2)}) collective-permute-start(bf16[64,2,66,1]{2,0,3,1:T(8,128)(2,1)S(1)} %copy.101), channel_id=1, source_target_pairs={{0,1},{2,3},{4,5},{6,7},{8,9},{10,11},{12,13},{14,15},{16,17},{18,... | collective-permute-start | bytes 50696 | tf_op jit(solution)/shard_map/ppermute | solution.py:17
  226.4 11.8 %collective-permute-start.7 = (bf16[64,2,66,1]{2,0,3,1:T(8,128)(2,1)S(1)}, bf16[64,2,66,1]{2,0,3,1:T(8,128)(2,1)S(1)}, u32[]{:S(2)}, u32[]{:S(2)}) collective-permute-start(bf16[64,2,66,1]{2,0,3,1:T(8,128)(2,1)S(1)} %copy.102), channel_id=1, source_target_pairs={{1,0},{3,2},{5,4},{7,6},{9,8},{11,10},{13,12},{15,14},{17,16},{19,... | collective-permute-start | bytes 50696 | tf_op jit(solution)/shard_map/ppermute | solution.py:18
  333.2 15.4 %copy-start.29 = (bf16[27,64,64]{2,1,0:T(8,128)(2,1)S(1)}, bf16[27,64,64]{2,1,0:T(8,128)(2,1)}, u32[]{:S(2)}) copy-start(bf16[27,64,64]{2,1,0:T(8,128)(2,1)} %param.12) | copy-start | bytes 663556
  348.6 11.2 %copy-start.22 = (bf16[1,64,2,64,256]{4,1,3,2,0:T(8,128)(2,1)S(1)}, bf16[1,64,2,64,256]{4,1,3,2,0:T(8,128)(2,1)}, u32[]{:S(2)}) copy-start(bf16[1,64,2,64,256]{4,1,3,2,0:T(8,128)(2,1)} %get-tuple-element.27) | copy-start | bytes 12582916
  404.2 10.4 %copy-start.15 = (bf16[1,64,2,64,256]{4,1,3,2,0:T(8,128)(2,1)S(1)}, bf16[1,64,2,64,256]{4,1,3,2,0:T(8,128)(2,1)}, u32[]{:S(2)}) copy-start(bf16[1,64,2,64,256]{4,1,3,2,0:T(8,128)(2,1)} %get-tuple-element.20) | copy-start | bytes 12582916
  435.9 10.5 %copy-start.11 = (bf16[1,64,2,64,256]{4,1,3,2,0:T(8,128)(2,1)S(1)}, bf16[1,64,2,64,256]{4,1,3,2,0:T(8,128)(2,1)}, u32[]{:S(2)}) copy-start(bf16[1,64,2,64,256]{4,1,3,2,0:T(8,128)(2,1)} %get-tuple-element.16) | copy-start | bytes 12582916
  436.0 10.4 %copy-start.12 = (bf16[1,64,2,64,256]{4,1,3,2,0:T(8,128)(2,1)S(1)}, bf16[1,64,2,64,256]{4,1,3,2,0:T(8,128)(2,1)}, u32[]{:S(2)}) copy-start(bf16[1,64,2,64,256]{4,1,3,2,0:T(8,128)(2,1)} %get-tuple-element.17) | copy-start | bytes 12582916
  490.1 93.3 %copy-start.1 = (bf16[27,64]{1,0:T(8,128)(2,1)S(1)}, bf16[27,64]{1,0:T(8,128)(2,1)}, u32[]{:S(2)}) copy-start(bf16[27,64]{1,0:T(8,128)(2,1)} %param.13) | copy-start | bytes 10372
  (23 other events, 189.6 us)
Sparse Core Ops, SparseCore 0:
  11.5 10.3 reduce-scatter.3
  24.8 8.8 reduce-scatter.5
  111.9 5.4 reduce-scatter.7
  490.3 90.9 all-reduce.3
where the time goes:
time: 596 us; the launch traced here: 590 us
  matrix products  207 us (35%)
  local copies, waits for them, and re-layouts  121 us (20%)
  waiting for transfers between devices  93.5 us (16%)
  blocking collectives  60 us (10%)
  other arithmetic  56.7 us (10%)
  starting transfers between devices  36.9 us (6%)
  between operations  14.8 us (2%)
    dot_general x9, matrix products, shards(): jnp.einsum('izxy,dozxy->dio', act_in, stacked, preferred_element_type=jnp...  90.2 us
    another operation x4, local copies, waits for them, and re-layouts, shifted_windows(): return jnp.stack(windows, axis=0)  78.2 us
    psum x1, waiting for transfers between devices, shards(): lax.psum((grad_first, grad_second), ('wide', 'narrow'))  61.7 us
    psum x1, blocking collectives, shards(): lax.psum((grad_first, grad_second), ('wide', 'narrow'))  60 us
    dot_general x9, matrix products, shards(): jnp.einsum('dio,dozxy->izxy', w_first[plane_index::9], stacked, preferred...  53.7 us
    convert_element_type x1, other arithmetic, shards(): return (grad_in.astype(jnp.bfloat16), grad_first, grad_second)  25 us
    concatenate x6, other arithmetic, with_halo(): x = jnp.concatenate([before, x, after], axis=dim)  19.9 us
    unnamed x95, local copies, waits for them, and re-layouts  19.5 us
  transfers between devices with their start and end apart: 16, of which 10 were waited for; matrix products, arithmetic and copies ran while one was open for 12% of the time, Pallas kernels for 0%

commit v1 on v0

--- a/solution.py
+++ b/solution.py
@@ -1,10 +1,500 @@
+import functools
+
 import jax
 import jax.numpy as jnp
+import ml_dtypes
+import numpy as np
 from jax import lax
+from jax.experimental import pallas as pl
+from jax.experimental.pallas import tpu as pltpu
 from jax.sharding import PartitionSpec as P
 
 two_pi = 6.283185307179586
 highest = lax.Precision.HIGHEST
+bf16 = jnp.bfloat16
+f32 = jnp.float32
+
+
+def split_table(table):
+    high = table.astype(np.float32).astype(ml_dtypes.bfloat16)
+    low = (table - high.astype(np.float64)).astype(np.float32).astype(ml_dtypes.bfloat16)
+    return np.stack([high, low])
+
+
+def cos_sin(left, right, length):
+    angles = (np.outer(left, right) % length) * (2.0 * np.pi / length)
+    return np.cos(angles), np.sin(angles)
+
+
+def y_table(wide, keep, half):
+    total = 2 * half
+    ky = np.arange(total)
+    rows = np.zeros(half + 128, np.int64)
+    used = np.zeros(half + 128)
+    rows[:half] = np.arange(half)
+    used[:half] = 1
+    for lane, y in ((0, half), (1, half + 1), (127, -1), (126, -2)):
+        rows[half + lane] = y
+        used[half + lane] = 1
+    cos, sin = cos_sin(rows, ky, total)
+    cos, sin = cos * used[:, None], -sin * used[:, None]
+    shape = (half + 128, wide, 2, keep)
+    both = np.stack([cos.reshape(shape), sin.reshape(shape)], axis=2)
+    return split_table(both.reshape(half + 128, wide * 4 * keep))
+
+
+def x_table(total):
+    index = np.arange(total)
+    cos, sin = cos_sin(index, index, total)
+    return split_table(np.concatenate([cos, sin], axis=0))
+
+
+def dot(a, b):
+    return jnp.dot(a, b, preferred_element_type=f32)
+
+
+def dot_nt(a, b):
+    return lax.dot_general(a, b, (((1,), (1,)), ((), ())), preferred_element_type=f32)
+
+
+def parts_of(x):
+    high = x.astype(bf16)
+    return high, (x - high.astype(f32)).astype(bf16)
+
+
+def lanes_of(shape):
+    return lax.broadcasted_iota(jnp.int32, shape, len(shape) - 1)
+
+
+def forward_y_kernel(index_ref, own_ref, other_ref, table_ref, out_ref):
+    slices, rows, half = own_ref.shape
+    wide = out_ref.shape[0]
+    narrow = index_ref[0]
+    stacked = jnp.concatenate(
+        [own_ref[...].reshape(slices * rows, half), other_ref[...].reshape(slices * rows, half)],
+        axis=0,
+    )
+    high, low = parts_of(stacked)
+    t_high = table_ref[0, :half, :]
+    t_low = table_ref[1, :half, :]
+    total = dot(high, t_high) + dot(low, t_high) + dot(high, t_low)
+    lane = lanes_of((1, 128))
+    sign = (1 - 2 * (lane % 2)).astype(f32)
+    own_scale = jnp.where(narrow == 0, 1.0, sign)
+    other_scale = jnp.where(narrow == 0, sign, 1.0)
+    first = (lane // 32) % 2 == 0
+    count = slices * rows
+    for w in range(wide):
+        cols = slice(128 * w, 128 * (w + 1))
+        merged = total[:count, cols] * own_scale + total[count:, cols] * other_scale
+        z0 = merged[:rows]
+        z1 = merged[rows:]
+        as_zero = jnp.where(first, z0, pltpu.roll(z1, 32, 1))
+        as_one = jnp.where(first, pltpu.roll(z0, 96, 1), z1)
+        out_ref[w] = jnp.where(narrow == 0, as_zero, as_one)
+
+
+def forward_y(index, own, other, table, wide):
+    slices, rows, half = own.shape
+    return pl.pallas_call(
+        forward_y_kernel,
+        out_shape=jax.ShapeDtypeStruct((wide, rows, 128), f32),
+        in_specs=[pl.BlockSpec(memory_space=pltpu.SMEM)] + [pl.BlockSpec(memory_space=pltpu.VMEM)] * 3,
+        out_specs=pl.BlockSpec(memory_space=pltpu.VMEM),
+        compiler_params=pltpu.CompilerParams(vmem_limit_bytes=40 << 20),
+        name="forward_y",
+    )(index, own, other, table)
+
+
+def along_x_kernel(in_ref, table_ref, weight_ref, out_ref, line_ref):
+    wide, rows, lanes = in_ref.shape
+    total = wide * rows
+    held = out_ref.shape[1]
+    lane = lanes_of((1, lanes))
+    sign = jnp.where(lane < 64, 1.0, -1.0)
+    t_high = table_ref[0]
+    t_low = table_ref[1]
+
+    def transform(value):
+        high, low = parts_of(value)
+        both = dot(t_high, jnp.concatenate([high, low], axis=1))
+        return both[:, :lanes] + both[:, lanes:] + dot(t_low, high)
+
+    spread = transform(in_ref[...].reshape(total, lanes))
+    spectrum = spread[:total] + sign * pltpu.roll(spread[total:], 64, 1)
+    back = transform(spectrum * weight_ref[...])
+    line_ref[:8] = jnp.zeros((8, lanes), f32)
+    line_ref[8 + total :] = jnp.zeros((8, lanes), f32)
+    line_ref[8 : 8 + total] = back[:total] - sign * pltpu.roll(back[total:], 64, 1)
+    for w in range(wide):
+        out_ref[w] = line_ref[6 + rows * w : 6 + rows * w + held]
+
+
+def along_x(pieces, table, weight_lines):
+    wide, rows, lanes = pieces.shape
+    return pl.pallas_call(
+        along_x_kernel,
+        out_shape=jax.ShapeDtypeStruct((wide, rows + 8, lanes), f32),
+        in_specs=[pl.BlockSpec(memory_space=pltpu.VMEM)] * 3,
+        out_specs=pl.BlockSpec(memory_space=pltpu.VMEM),
+        scratch_shapes=[pltpu.VMEM((wide * rows + 16, lanes), f32)],
+        compiler_params=pltpu.CompilerParams(vmem_limit_bytes=40 << 20),
+        name="along_x",
+    )(pieces, table, weight_lines)
+
+
+def masked_kernel(
+    scale,
+    index_ref,
+    own_ref,
+    other_ref,
+    table_ref,
+    taps_ref,
+    pick_ref,
+    top_ref,
+    bottom_ref,
+    in_hbm,
+    mid_hbm,
+    side_hbm,
+    shifted_hbm,
+    pay_ref,
+    noise_ref,
+    in_ref,
+    mid_ref,
+    side_ref,
+    shifted_ref,
+    sum_ref,
+    second_ref,
+    sems,
+):
+    wide, held, lanes = own_ref.shape
+    rows = held - 8
+    groups = rows // 8
+    half = mid_ref.shape[1]
+    ext = half + 128
+    narrow = index_ref[0]
+    copies = [
+        pltpu.make_async_copy(mid_hbm, mid_ref, sems.at[0]),
+        pltpu.make_async_copy(side_hbm, side_ref, sems.at[1]),
+        pltpu.make_async_copy(in_hbm, in_ref, sems.at[2]),
+    ]
+    for copy in copies:
+        copy.start()
+
+    lane = lanes_of((1, lanes))
+    sign = jnp.where(narrow == 0, 1.0, (1 - 2 * (lane % 2)).astype(f32))
+    first = (lane // 32) % 2 == 0
+    z_lines = ([], [])
+    for w in range(wide):
+        own = own_ref[w] * sign
+        other = other_ref[w] * sign
+        even = jnp.where(narrow == 0, own, other)
+        odd = jnp.where(narrow == 0, other, own)
+        z_lines[0].append(jnp.where(first, even, pltpu.roll(odd, 32, 1)))
+        z_lines[1].append(jnp.where(first, pltpu.roll(even, 96, 1), odd))
+    lines = jnp.concatenate(
+        [jnp.concatenate(z_lines[0], axis=1), jnp.concatenate(z_lines[1], axis=1)], axis=0
+    )
+    high, low = parts_of(lines)
+    noise = dot_nt(high, table_ref[0]) + dot_nt(low, table_ref[0]) + dot_nt(high, table_ref[1])
+    column = lanes_of((1, ext))
+    beside = jnp.where(narrow == 0, column - half, ext - 1 - column) < 2
+    ours = (column < half) | beside
+    noise = jnp.where(ours, noise * scale, 0.0).astype(bf16).astype(f32)
+    for d in range(3):
+        moved = noise if d == 1 else pltpu.roll(noise, (d - 1) % ext, 1)
+        for z in range(2):
+            noise_ref[d, z] = moved[z * held : (z + 1) * held]
+
+    copies[0].wait()
+    copies[1].wait()
+    side_ok = lane == jnp.where(narrow == 0, 0, 127)
+
+    def window_of(start):
+        pieces = [noise_ref[d, z, pl.ds(start, 16), :] for z in range(2) for d in range(3)]
+        return jnp.concatenate(pieces + [jnp.zeros((32, ext), f32)], axis=0)
+
+    def store_row(window, tap_row, mask, side, row):
+        value = dot(taps_ref[pl.ds(tap_row * 128, 128), :], window)
+        main = jnp.where(mask.astype(f32) > 0, value[:, :half], 0.0)
+        edge = jnp.where((side.astype(f32) > 0) & side_ok, value[:, half:], 0.0)
+        whole = jnp.concatenate([main, edge], axis=1)
+        where = pl.ds(pl.multiple_of(row * 128, 128), 128)
+        for d in range(3):
+            moved = whole if d == 1 else pltpu.roll(whole, (d - 1) % ext, 1)
+            shifted_ref[d, where, :] = moved[:, :half].astype(bf16)
+
+    second_ref[...] = jnp.zeros_like(second_ref)
+
+    def group_body(g, carry):
+        start = pl.multiple_of(g * 8, 8)
+        wide_window = window_of(start)
+        window = wide_window.astype(bf16)
+        turned = wide_window[:, :half].T.astype(bf16)
+        here = pl.ds(pl.multiple_of(g * 1024, 1024), 1024)
+        second_ref[...] += dot(mid_ref[here, :], turned)
+        for m in range(8):
+            spot = pl.ds(pl.multiple_of(g * 1024 + m * 128, 128), 128)
+            store_row(window, m + 1, mid_ref[spot, :], side_ref[spot, :], g * 8 + m + 1)
+        return carry
+
+    lax.fori_loop(0, groups, group_body, 0)
+    window = window_of(0).astype(bf16)
+    store_row(window, 0, top_ref[:, :half], top_ref[:, half:], 0)
+    window = window_of(rows - 8).astype(bf16)
+    store_row(window, 9, bottom_ref[:, :half], bottom_ref[:, half:], rows + 1)
+    outs = [
+        pltpu.make_async_copy(shifted_ref.at[d], shifted_hbm.at[d], sems.at[3 + d])
+        for d in range(3)
+    ]
+    for copy in outs:
+        copy.start()
+
+    copies[2].wait()
+    sum_ref[...] = jnp.zeros_like(sum_ref)
+
+    def chunk_body(k, carry):
+        right = in_ref[pl.ds(pl.multiple_of(k * 4 * half, 4 * half), 4 * half), :]
+        for d in range(3):
+            left = jnp.concatenate(
+                [
+                    shifted_ref[d, pl.ds(pl.multiple_of(k * 1024 + 256 * q, 256), 512), :]
+                    for q in range(4)
+                ],
+                axis=1,
+            )
+            sum_ref[d] += dot(left, right)
+        return carry
+
+    lax.fori_loop(0, groups, chunk_body, 0)
+
+    singles = []
+    for d in range(3):
+        for dx in range(3):
+            total = None
+            for par in range(2):
+                i4 = par + 2 - dx
+                block = sum_ref[d, i4 * 128 : (i4 + 1) * 128, par * 128 : (par + 1) * 128]
+                total = block if total is None else total + block
+            turned = total.T
+            upper = turned[:64]
+            lower = turned[64:]
+            slot = d * 3 + dx
+            pay_ref[slot * 64 : (slot + 1) * 64] = jnp.where(lane < 64, lower, upper)
+            singles.append(upper + pltpu.roll(lower, 64, 1))
+    pieces = [
+        second_ref[(m * 2 + z) * 64 : (m * 2 + z + 1) * 64, :] for m in range(8) for z in range(2)
+    ]
+    second = jnp.dot(
+        jnp.concatenate(pieces, axis=1), pick_ref[...], preferred_element_type=f32, precision=highest
+    )
+    singles.append(second)
+    for k in range(5):
+        pay_ref[(9 + k) * 64 : (10 + k) * 64] = jnp.where(
+            lane < 64, singles[2 * k], pltpu.roll(singles[2 * k + 1], 64, 1)
+        )
+    for copy in outs:
+        copy.wait()
+
+
+def masked_and_kernels(index, own, other, table, taps, pick, top, bottom, lines_in, mid, side, scale):
+    wide, held, lanes = own.shape
+    rows = held - 8
+    half = mid.shape[1]
+    ext = half + 128
+    vmem = pl.BlockSpec(memory_space=pltpu.VMEM)
+    anywhere = pl.BlockSpec(memory_space=pl.ANY)
+    return pl.pallas_call(
+        functools.partial(masked_kernel, scale),
+        out_shape=(
+            jax.ShapeDtypeStruct((3, (rows + 2) * 128, half), bf16),
+            jax.ShapeDtypeStruct((14 * 64, 128), f32),
+        ),
+        in_specs=[pl.BlockSpec(memory_space=pltpu.SMEM)] + [vmem] * 7 + [anywhere] * 3,
+        out_specs=(anywhere, vmem),
+        scratch_shapes=[
+            pltpu.VMEM((3, 2, held, ext), f32),
+            pltpu.VMEM(lines_in.shape, bf16),
+            pltpu.VMEM(mid.shape, bf16),
+            pltpu.VMEM(side.shape, bf16),
+            pltpu.VMEM((3, (rows + 2) * 128, half), bf16),
+            pltpu.VMEM((3, 512, 256), f32),
+            pltpu.VMEM((1024, 128), f32),
+            pltpu.SemaphoreType.DMA((6,)),
+        ],
+        compiler_params=pltpu.CompilerParams(vmem_limit_bytes=56 << 20),
+        name="masked_and_kernels",
+    )(index, own, other, table, taps, pick, top, bottom, lines_in, mid, side)
+
+
+def input_kernel(shifted_hbm, weight_ref, out_hbm, shifted_ref, out_ref, in_sems, out_sems):
+    rows = out_ref.shape[0] // 128
+    groups = rows // 8
+    chunk = 8 * 128
+    copies = []
+    for g in range(groups):
+        first = 0 if g == 0 else chunk * g + 256
+        last = chunk * (g + 1) + 256
+        copies.append(
+            [
+                pltpu.make_async_copy(
+                    shifted_hbm.at[d, first:last], shifted_ref.at[d, first:last], in_sems.at[g, d]
+                )
+                for d in range(3)
+            ]
+        )
+    for group in copies:
+        for copy in group:
+            copy.start()
+    outs = []
+    for g in range(groups):
+        for copy in copies[g]:
+            copy.wait()
+
+        def pair(q, carry, g=g):
+            row = pl.multiple_of(g * chunk + q * 256, 256)
+            stacked = jnp.concatenate(
+                [shifted_ref[d, pl.ds(row, 512), :] for d in range(3)], axis=0
+            )
+            out_ref[pl.ds(row, 256), :] = dot(weight_ref[...], stacked).astype(bf16)
+            return carry
+
+        lax.fori_loop(0, 4, pair, 0)
+        span = slice(g * chunk, (g + 1) * chunk)
+        copy = pltpu.make_async_copy(out_ref.at[span], out_hbm.at[span], out_sems.at[g])
+        copy.start()
+        outs.append(copy)
+    for copy in outs:
+        copy.wait()
+
+
+def input_gradient(shifted, weight):
+    taps, count, half = shifted.shape
+    rows = count // 128 - 2
+    anywhere = pl.BlockSpec(memory_space=pl.ANY)
+    return pl.pallas_call(
+        input_kernel,
+        out_shape=jax.ShapeDtypeStruct((rows * 128, half), bf16),
+        in_specs=[anywhere, pl.BlockSpec(memory_space=pltpu.VMEM)],
+        out_specs=anywhere,
+        scratch_shapes=[
+            pltpu.VMEM(shifted.shape, bf16),
+            pltpu.VMEM((rows * 128, half), bf16),
+            pltpu.SemaphoreType.DMA((rows // 8, 3)),
+            pltpu.SemaphoreType.DMA((rows // 8,)),
+        ],
+        cost_estimate=pl.CostEstimate(
+            flops=2 * rows * 128 * half * 1536, bytes_accessed=4 * rows * 128 * half * 2, transcendentals=0
+        ),
+        compiler_params=pltpu.CompilerParams(vmem_limit_bytes=40 << 20),
+        name="input_gradient",
+    )(shifted, weight)
+
+
+def tap_choice():
+    choice = np.zeros((27, 10, 2, 128), np.float32)
+    for dz in (-1, 0, 1):
+        for dx in (-1, 0, 1):
+            for dy in (-1, 0, 1):
+                tap = (dz + 1) * 9 + (dx + 1) * 3 + dy + 1
+                for m in range(-1, 9):
+                    for z in range(2):
+                        if 0 <= z - dz < 2:
+                            r = m + 2 - dx
+                            choice[tap, m + 1, z, ((z - dz) * 3 + dy + 1) * 16 + r] = 1
+    return choice
+
+
+def kernel_matrix(w_first):
+    channels = w_first.shape[1]
+    w = w_first.reshape(3, 3, 3, channels, channels)
+    grid = jnp.stack([jnp.stack([w[1], w[0]]), jnp.stack([w[2], w[1]])])
+    grid = grid.transpose(2, 3, 0, 4, 1, 5).reshape(3, 3, 128, 128)
+    none = jnp.zeros((3, 128, 128), w.dtype)
+    row0 = jnp.stack([grid[2], grid[1], grid[0], none], axis=2)
+    row1 = jnp.stack([none, grid[2], grid[1], grid[0]], axis=2)
+    both = jnp.stack([row0, row1])
+    return both.transpose(0, 2, 1, 3, 4).reshape(256, 1536)
+
+
+def fast(denoised, clean_volume, weight, act_in, act_mid, w_first, w_second):
+    wide = lax.axis_size("wide")
+    slices, rows, half = denoised.shape
+    channels = act_in.shape[0]
+    keep = weight.shape[0]
+    total_x = wide * rows
+    total_y = 2 * half
+    narrow = lax.axis_index("narrow")
+    index = narrow.astype(jnp.int32).reshape(1)
+    swap = [(0, 1), (1, 0)]
+    table_y = jnp.asarray(y_table(wide, keep, half))
+    table_x = jnp.asarray(x_table(total_x))
+
+    error = denoised - clean_volume
+    error_other = lax.ppermute(error, "narrow", swap)
+    lines = forward_y(index, error, error_other, table_y, wide)
+    lines = lax.all_to_all(lines, "wide", 0, 0, tiled=True)
+
+    mid = act_mid.transpose(2, 1, 0, 3).reshape(rows * 128, half)
+    edge = jnp.where(narrow == 0, act_mid[..., half - 128 :], act_mid[..., :128])
+    side = lax.ppermute(edge, "narrow", swap).transpose(2, 1, 0, 3).reshape(rows * 128, 128)
+    first = jnp.concatenate([mid[:128], side[:128]], axis=1)
+    last = jnp.concatenate([mid[-128:], side[-128:]], axis=1)
+    up = [(i, i + 1) for i in range(wide - 1)]
+    top = lax.ppermute(last, "wide", up)
+    bottom = lax.ppermute(first, "wide", [(j, i) for i, j in up])
+    lines_in = act_in.reshape(channels, slices, rows // 2, 2, half)
+    lines_in = lines_in.transpose(2, 4, 3, 1, 0).reshape(rows // 2 * half, 256)
+
+    weight_lines = jnp.tile(weight.T, (1, 4))
+    lines = along_x(lines, table_x, weight_lines)
+    lines = lax.all_to_all(lines, "wide", 0, 0, tiled=True)
+    lines_other = lax.ppermute(lines, "narrow", swap)
+
+    choice = tap_choice()
+    taps = jnp.einsum(
+        "tc,tmzk->mzck", w_second, jnp.asarray(choice, bf16), preferred_element_type=f32
+    )
+    taps = taps.astype(bf16).reshape(1280, 128)
+    pick = np.zeros((16 * 128, 128), np.float32)
+    pick[:, :27] = choice[:, 1:9].reshape(27, 16 * 128).T
+    shifted, pay = masked_and_kernels(
+        index,
+        lines,
+        lines_other,
+        table_y,
+        taps,
+        jnp.asarray(pick),
+        top,
+        bottom,
+        lines_in,
+        mid,
+        side,
+        -2.0 / (total_x * total_y),
+    )
+    grad_in = input_gradient(shifted, kernel_matrix(w_first))
+    grad_in = grad_in.reshape(rows, slices, channels, half).transpose(2, 1, 0, 3)
+
+    count = pay.shape[0] // 2
+    mine = lax.dynamic_slice_in_dim(pay, narrow * count, count, 0)
+    theirs = lax.dynamic_slice_in_dim(pay, (1 - narrow) * count, count, 0)
+    mine = mine + lax.ppermute(theirs, "narrow", swap)
+    mine = mine.reshape(wide, count // wide, 128)
+    mine = lax.all_to_all(mine, "wide", 0, 0, tiled=True)
+    mine = jnp.broadcast_to(mine.sum(axis=0, keepdims=True), mine.shape)
+    mine = lax.all_to_all(mine, "wide", 0, 0, tiled=True).reshape(count, 128)
+    theirs = lax.ppermute(mine, "narrow", swap)
+    pay = jnp.concatenate(
+        [jnp.where(narrow == 0, mine, theirs), jnp.where(narrow == 0, theirs, mine)], axis=0
+    )
+    pay = pay.reshape(14, 64, 2, 64)
+    outer = pay[:9].reshape(3, 3, 64, 2, 64)
+    inner = pay[9:].transpose(0, 2, 1, 3).reshape(10, 64, 64)
+    grad_second = inner[9, :, :27].T
+    inner = inner[:9].reshape(3, 3, 64, 64)
+    grad_first = jnp.stack([outer[:, :, :, 1], inner, outer[:, :, :, 0]])
+    grad_first = grad_first.transpose(0, 2, 1, 3, 4).reshape(27, channels, channels)
+    return (grad_in, grad_first, grad_second)
 
 
 def with_halo(x, sides, width):
@@ -43,7 +533,7 @@
     return jnp.stack(windows, axis=0)
 
 
-def shards(denoised, clean_volume, weight, act_in, act_mid, w_first, w_second):
+def plain(denoised, clean_volume, weight, act_in, act_mid, w_first, w_second):
     wide_count = lax.axis_size("wide")
     narrow_count = lax.axis_size("narrow")
     slices, rows_x, half_cols = denoised.shape
@@ -153,6 +643,18 @@
     return (grad_in.astype(jnp.bfloat16), grad_first, grad_second)
 
 
+def shards(denoised, clean_volume, weight, act_in, act_mid, w_first, w_second):
+    sizes = (
+        lax.axis_size("wide"),
+        lax.axis_size("narrow"),
+        *denoised.shape,
+        weight.shape[0],
+        act_in.shape[0],
+    )
+    chosen = fast if sizes == (8, 2, 2, 64, 256, 32, 64) else plain
+    return chosen(denoised, clean_volume, weight, act_in, act_mid, w_first, w_second)
+
+
 def solution(mesh):
     placed = (
         P("grp", "wide", "narrow"),

time: 596 us -> 159 us (0.27)
  matrix products: 207 us -> 1.03 us
  local copies, waits for them, and re-layouts: 121 us -> 50.6 us
  blocking collectives: 60 us -> 0 us
  waiting for transfers between devices: 93.5 us -> 34.3 us
  other arithmetic: 56.7 us -> 8.38 us
  Pallas kernels: 0 us -> 38.1 us
  between operations: 14.8 us -> 1.08 us
  starting transfers between devices: 36.9 us -> 24.1 us
    dot_general x32 -> x1, matrix products: 207 us -> 1.03 us  [fast(): jnp.einsum('tc,tmzk->mzck', w_second, jnp.asarray(choice, bf16), preferre...]
    another operation x5 -> x6, local copies, waits for them, and re-layouts: 80.6 us -> 0.54 us  [the longest x3 0.38 us: kernel_matrix(): row0 = jnp.stack([grid[2], grid[1], grid[0], none], axis=2)]
    psum x1 -> x0, waiting for transfers between devices: 61.7 us -> none  [shards(): lax.psum((grad_first, grad_second), ('wide', 'narrow'))]
    psum x1 -> x0, blocking collectives: 60 us -> none  [shards(): lax.psum((grad_first, grad_second), ('wide', 'narrow'))]
    pallas_call x0 -> x4, Pallas kernels: none -> 38.1 us  [the longest x1 20.4 us: masked_and_kernels(): pl.pallas_call(functools.partial(masked_kernel, scale), out_shape=(jax.Sh...]
    convert_element_type x2 -> x0, other arithmetic: 26.1 us -> none  [the longest x1 25 us: shards(): return (grad_in.astype(jnp.bfloat16), grad_first, grad_second)]
    reshape x8 -> x6, local copies, waits for them, and re-layouts: 0.58 us -> 21.8 us  [the longest x2 10.3 us: fast(): lines_in = act_in.reshape(channels, slices, rows // 2, 2, half)]
    concatenate x6 -> x3, other arithmetic: 19.9 us -> 0.05 us  [the longest x1 0.02 us: fast(): jnp.concatenate([jnp.where(narrow == 0, mine, theirs), jnp.where(narrow =...]
  transfers between devices with their start and end apart: 16 -> 11, of which waited for: 10 -> 6; matrix products, arithmetic and copies ran while one was open for 12% -> 30% of each run, Pallas kernels for 0% -> 11%
where the time goes in v1:
time: 159 us; the launch traced here: 158 us
  local copies, waits for them, and re-layouts  50.6 us (32%)
  Pallas kernels  38.1 us (24%)
  waiting for transfers between devices  34.3 us (22%)
  starting transfers between devices  24.1 us (15%)
  other arithmetic  8.38 us (5%)
    pallas_call x1, Pallas kernels, masked_and_kernels(): pl.pallas_call(functools.partial(masked_kernel, scale), out_shape=(jax.Sh...  20.4 us
    all_to_all x2, waiting for transfers between devices, fast(): lines = lax.all_to_all(lines, 'wide', 0, 0, tiled=True)  17.5 us
    pallas_call x1, Pallas kernels, input_gradient(): pl.pallas_call(input_kernel, out_shape=jax.ShapeDtypeStruct((rows * 128,...  14.1 us
    all_to_all x2, starting transfers between devices, fast(): lines = lax.all_to_all(lines, 'wide', 0, 0, tiled=True)  10.5 us
    reshape x2, local copies, waits for them, and re-layouts, fast(): lines_in = act_in.reshape(channels, slices, rows // 2, 2, half)  10.3 us
    unnamed x28, local copies, waits for them, and re-layouts  9.38 us
    transpose x1, local copies, waits for them, and re-layouts, fast(): mid = act_mid.transpose(2, 1, 0, 3).reshape(rows * 128, half)  6.55 us
    reshape x1, local copies, waits for them, and re-layouts, fast(): lines_in = lines_in.transpose(2, 4, 3, 1, 0).reshape(rows // 2 * half, 256)  6.38 us
  transfers between devices with their start and end apart: 11, of which 6 were waited for; matrix products, arithmetic and copies ran while one was open for 30% of the time, Pallas kernels for 11%

profile of v1, /device:TPU:0, one launch (start us, length us, event | category | flops | bytes accessed | tf_op | source)
XLA Modules:
  0.0 157.5 jit_solution(6739926696653069129)
XLA Ops:
  0.7 3.9 %slice_select_fusion = bf16[64,2,64,128]{3,2,1,0:T(8,128)(2,1)} fusion(bf16[64,2,64,256]{3,2,1,0:T(8,128)(2,1)} %param.15, pred[]{:T(512)S(6)} %eq.2), kind=kLoop, calls=%fused_computation.1 | loop fusion | flops 1048576 | bytes 6291457 | tf_op jit(solution)/shard_map/jit(_where)/select_n | solution.py:439
  5.2 3.7 %collective-permute-done.other_ref = f32[2,64,256]{2,1,0:T(8,128)S(1)} collective-permute-done((f32[2,64,256]{2,1,0:T(8,128)S(1)}, f32[2,64,256]{2,1,0:T(8,128)S(1)}, u32[]{:S(2)}, u32[]{:S(2)}) %collective-permute-start) | collective-permute-done | bytes 131104 | tf_op jit(solution)/shard_map/ppermute | solution.py:434
  10.3 6.9 %all-to-all-start = ((f32[8,64,128]{2,1,0:T(8,128)}), f32[8,64,128]{2,1,0:T(8,128)S(1)}, u32[]{:S(2)}, u32[]{:S(2)}) async-start(f32[8,64,128]{2,1,0:T(8,128)} %forward_y.1), calls=%async_computation | async-start | bytes 524288 | tf_op jit(solution)/shard_map/all_to_all | solution.py:436
  17.4 9.3 %all-to-all-done.in_ref = f32[8,64,128]{2,1,0:T(8,128)S(1)} async-done(((f32[8,64,128]{2,1,0:T(8,128)}), f32[8,64,128]{2,1,0:T(8,128)S(1)}, u32[]{:S(2)}, u32[]{:S(2)}) %all-to-all-start) | async-done | bytes 262176 | tf_op jit(solution)/shard_map/all_to_all | solution.py:436
  26.7 1.6 %copy-done.3 = bf16[2,1024,512]{2,1,0:T(8,128)(2,1)S(1)} copy-done((bf16[2,1024,512]{2,1,0:T(8,128)(2,1)S(1)}, bf16[2,1024,512]{2,1,0:T(8,128)(2,1)}, u32[]{:S(2)}) %copy-start.3) | copy-done | bytes 2097176
  28.3 2.2 %along_x.1 = f32[8,72,128]{2,1,0:T(8,128)} custom-call(f32[8,64,128]{2,1,0:T(8,128)S(1)} %all-to-all-done.in_ref, bf16[2,1024,512]{2,1,0:T(8,128)(2,1)S(1)} %copy-done.3, f32[512,128]{1,0:T(8,128)S(1)} %copy.44.weight_ref), custom_call_target="tpu_custom_call" | custom-call | tf_op jit(solution)/shard_map/along_x/pallas_call | solution.py:135
  30.5 3.6 %all-to-all-start.1 = ((f32[8,72,128]{2,1,0:T(8,128)}), f32[8,72,128]{2,1,0:T(8,128)S(1)}, u32[]{:S(2)}, u32[]{:S(2)}) async-start(f32[8,72,128]{2,1,0:T(8,128)} %along_x.1), calls=%async_computation.1 | async-start | bytes 589824 | tf_op jit(solution)/shard_map/all_to_all | solution.py:451
  35.5 8.2 %all-to-all-done.1.own_ref = f32[8,72,128]{2,1,0:T(8,128)S(1)} async-done(((f32[8,72,128]{2,1,0:T(8,128)}), f32[8,72,128]{2,1,0:T(8,128)S(1)}, u32[]{:S(2)}, u32[]{:S(2)}) %all-to-all-start.1) | async-done | bytes 294944 | tf_op jit(solution)/shard_map/all_to_all | solution.py:451
  45.1 3.3 %collective-permute-start.3 = (bf16[128,384]{1,0:T(8,128)(2,1)S(1)}, bf16[128,384]{1,0:T(8,128)(2,1)S(1)}, u32[]{:S(2)}, u32[]{:S(2)}) collective-permute-start(bf16[128,384]{1,0:T(8,128)(2,1)S(1)} %pad_maximum_fusion.1), channel_id=1, source_target_pairs={{0,2},{2,4},{4,6},{6,8},{8,10},{10,12},{12,14},{1,3},{3,5},{5,7},{... | collective-permute-start | bytes 294920 | tf_op jit(solution)/shard_map/ppermute | solution.py:444
  50.8 6.5 %copy.50 = bf16[64,2,64,256]{3,2,1,0:T(8,128)(2,1)} copy(bf16[64,2,64,256]{3,0,1,2:T(8,128)(2,1)} %bitcast.67) | data formatting | bytes 8388608 | tf_op jit(solution)/shard_map/transpose | solution.py:438
  57.4 7.2 %reshape.71 = bf16[64,2,32,2,256]{4,3,2,1,0:T(2,128)(2,1)} reshape(bf16[64,2,64,256]{3,2,1,0:T(8,128)(2,1)} %param.14) | data formatting | bytes 8388608 | tf_op jit(solution)/shard_map/reshape | solution.py:446
  64.5 3.1 %copy.49 = bf16[64,2,32,2,256]{4,2,0,1,3:T(8,128)(2,1)S(1)} copy(bf16[64,2,32,2,256]{4,3,2,1,0:T(2,128)(2,1)} %reshape.71) | data formatting | bytes 8388608 | tf_op jit(solution)/shard_map/reshape | solution.py:446
  67.7 6.3 %copy.65 = bf16[32,8,32,256]{3,1,2,0:T(8,128)(2,1)} copy(bf16[32,8,32,256]{3,2,1,0:T(8,128)(2,1)S(1)} %bitcast.68) | data formatting | bytes 8388608
  74.0 6.4 %copy.52.in_hbm = bf16[8192,256]{1,0:T(8,128)(2,1)} copy(bf16[8192,256]{0,1:T(8,128)(2,1)} %bitcast.69) | data formatting | bytes 8388608 | tf_op jit(solution)/shard_map/reshape | solution.py:447
  80.3 4.3 %copy.51 = bf16[64,2,64,128]{3,2,1,0:T(8,128)(2,1)} copy(bf16[64,2,64,128]{3,0,1,2:T(8,128)(2,1)} %bitcast.9) | data formatting | bytes 4194304 | tf_op jit(solution)/shard_map/transpose | solution.py:440
  85.4 20.4 %masked_and_kernels.1 = (bf16[3,8448,256]{2,1,0:T(8,128)(2,1)}, f32[896,128]{1,0:T(8,128)}) custom-call(s32[1]{0:T(128)} %bitcast.index_ref, f32[8,72,128]{2,1,0:T(8,128)} %copy-done.4, f32[8,72,128]{2,1,0:T(8,128)} %copy-done.6, bf16[2,384,1024]{2,1,0:T(8,128)(2,1)} %constant.24.clone.table_ref, bf16[1280,128]{1,0:T(8,128)(2,1)} %bitcast.73, ...), custom_call_target="tpu_custom_call" | custom-call | tf_op jit(solution)/shard_map/masked_and_kernels/pallas_call | solution.py:307
  108.3 1.7 %dynamic-slice_add_fusion = f32[448,128]{1,0:T(8,128)} fusion(f32[448,128]{1,0:T(8,128)S(1)} %collective-permute-done.5, f32[896,128]{1,0:T(8,128)} %get-tuple-element.6, s32[]{:T(128)S(6)} %select_n.29), kind=kLoop, calls=%fused_computation.11 | loop fusion | flops 57344 | bytes 688132 | tf_op jit(solution)/shard_map/add | solution.py:481
  110.0 4.8 %all-to-all-start.2 = ((f32[8,56,128]{2,1,0:T(8,128)}), f32[8,56,128]{2,1,0:T(8,128)S(1)}, u32[]{:S(2)}, u32[]{:S(2)}) async-start(f32[8,56,128]{2,1,0:T(8,128)} %bitcast.27), calls=%async_computation.2 | async-start | bytes 458752 | tf_op jit(solution)/shard_map/all_to_all | solution.py:483
  115.6 1.5 maximum_bitcast_fusion.5
  118.1 5.5 %all-to-all-done.2 = f32[8,56,128]{2,1,0:T(8,128)S(1)} async-done(((f32[8,56,128]{2,1,0:T(8,128)}), f32[8,56,128]{2,1,0:T(8,128)S(1)}, u32[]{:S(2)}, u32[]{:S(2)}) %all-to-all-start.2) | async-done | bytes 229408 | tf_op jit(solution)/shard_map/all_to_all | solution.py:483
  124.3 3.4 %all-to-all-start.3 = ((f32[8,56,128]{2,1,0:T(8,128)}), f32[8,56,128]{2,1,0:T(8,128)S(1)}, u32[]{:S(2)}, u32[]{:S(2)}) async-start(f32[8,56,128]{2,1,0:T(8,128)} %broadcast_in_dim.2), calls=%async_computation.3 | async-start | bytes 458752 | tf_op jit(solution)/shard_map/all_to_all | solution.py:485
  129.7 6.2 %all-to-all-done.3 = f32[8,56,128]{2,1,0:T(8,128)S(1)} async-done(((f32[8,56,128]{2,1,0:T(8,128)}), f32[8,56,128]{2,1,0:T(8,128)S(1)}, u32[]{:S(2)}, u32[]{:S(2)}) %all-to-all-start.3) | async-done | bytes 229408 | tf_op jit(solution)/shard_map/all_to_all | solution.py:485
  135.9 14.1 %input_gradient.1 = bf16[8192,256]{1,0:T(8,128)(2,1)S(1)} custom-call(bf16[3,8448,256]{2,1,0:T(8,128)(2,1)} %get-tuple-element.5.shifted_hbm, bf16[256,1536]{1,0:T(8,128)(2,1)S(1)} %reshape.75.weight_ref), custom_call_target="tpu_custom_call" | custom-call | flops 6442450944 | bytes 16777216 | tf_op jit(solution)/shard_map/input_gradient/pallas_call | solution.py:375
  150.0 4.4 %copy.67 = bf16[64,2,64,256]{3,0,1,2:T(8,128)(2,1)} copy(bf16[64,2,64,256]{3,2,1,0:T(8,128)(2,1)S(1)} %bitcast.65) | data formatting | bytes 8388608 | tf_op jit(solution)/shard_map/reshape | solution.py:476
  (79 shorter events, 17.9 us)
Async XLA Ops:
  0.6 49.1 %copy-start = (bf16[27,64]{1,0:T(8,128)(2,1)S(1)}, bf16[27,64]{1,0:T(8,128)(2,1)}, u32[]{:S(2)}) copy-start(bf16[27,64]{1,0:T(8,128)(2,1)} %param.17) | copy-start | bytes 10372
  0.6 8.3 %copy-start.2 = (bf16[2,384,1024]{2,1,0:T(8,128)(2,1)S(1)}, bf16[2,384,1024]{2,1,0:T(8,128)(2,1)}, u32[]{:S(2)}) copy-start(bf16[2,384,1024]{2,1,0:T(8,128)(2,1)} %constant.24.clone.table_ref) | copy-start | bytes 4718596
  0.7 4.4 %copy-start.8 = (f32[2,64,256]{2,1,0:T(8,128)S(1)}, f32[2,64,256]{2,1,0:T(8,128)}, u32[]{:S(2)}) copy-start(f32[2,64,256]{2,1,0:T(8,128)} %param.11) | copy-start | bytes 393220
  0.7 4.4 %copy-start.9 = (f32[2,64,256]{2,1,0:T(8,128)S(1)}, f32[2,64,256]{2,1,0:T(8,128)}, u32[]{:S(2)}) copy-start(f32[2,64,256]{2,1,0:T(8,128)} %param.12) | copy-start | bytes 393220
  0.7 16.5 %copy-start.12 = (f32[32,512]{1,0:T(8,128)S(1)}, f32[32,512]{1,0:T(8,128)}, u32[]{:S(2)}) copy-start(f32[32,512]{1,0:T(8,128)} %param.13) | copy-start | bytes 196612
  4.6 39.2 %collective-permute-start.2 = (bf16[64,2,64,128]{3,2,1,0:T(8,128)(2,1)}, bf16[64,2,64,128]{3,2,1,0:T(8,128)(2,1)}, u32[]{:S(2)}, u32[]{:S(2)}) collective-permute-start(bf16[64,2,64,128]{3,2,1,0:T(8,128)(2,1)} %slice_select_fusion), channel_id=1, source_target_pairs={{0,1},{1,0},{2,3},{3,2},{4,5},{5,4},{6,7},{7,6},{8,9},{9,8},{10,11... | collective-permute-start | bytes 6291464 | tf_op jit(solution)/shard_map/ppermute | solution.py:440
  5.1 3.9 %collective-permute-start = (f32[2,64,256]{2,1,0:T(8,128)S(1)}, f32[2,64,256]{2,1,0:T(8,128)S(1)}, u32[]{:S(2)}, u32[]{:S(2)}) collective-permute-start(f32[2,64,256]{2,1,0:T(8,128)S(1)} %sub.6.own_ref), channel_id=1, source_target_pairs={{0,1},{1,0},{2,3},{3,2},{4,5},{5,4},{6,7},{7,6},{8,9},{9,8},{10,11... | collective-permute-start | bytes 393224 | tf_op jit(solution)/shard_map/ppermute | solution.py:434
  8.9 40.8 %copy-start.7 = (bf16[27,10,2,128]{3,0,2,1:T(8,128)(2,1)S(1)}, bf16[27,10,2,128]{3,0,2,1:T(8,128)(2,1)}, u32[]{:S(2)}) copy-start(bf16[27,10,2,128]{3,0,2,1:T(8,128)(2,1)} %constant.26.clone) | copy-start | bytes 414724
  10.3 16.3 %all-to-all-start = ((f32[8,64,128]{2,1,0:T(8,128)}), f32[8,64,128]{2,1,0:T(8,128)S(1)}, u32[]{:S(2)}, u32[]{:S(2)}) async-start(f32[8,64,128]{2,1,0:T(8,128)} %forward_y.1), calls=%async_computation | async-start | bytes 524288 | tf_op jit(solution)/shard_map/all_to_all | solution.py:436
  26.7 1.6 %copy-start.3 = (bf16[2,1024,512]{2,1,0:T(8,128)(2,1)S(1)}, bf16[2,1024,512]{2,1,0:T(8,128)(2,1)}, u32[]{:S(2)}) copy-start(bf16[2,1024,512]{2,1,0:T(8,128)(2,1)} %constant.25.clone.table_ref) | copy-start | bytes 6291460
  30.5 13.3 %all-to-all-start.1 = ((f32[8,72,128]{2,1,0:T(8,128)}), f32[8,72,128]{2,1,0:T(8,128)S(1)}, u32[]{:S(2)}, u32[]{:S(2)}) async-start(f32[8,72,128]{2,1,0:T(8,128)} %along_x.1), calls=%async_computation.1 | async-start | bytes 589824 | tf_op jit(solution)/shard_map/all_to_all | solution.py:451
  43.8 13.6 %copy-start.4 = (f32[8,72,128]{2,1,0:T(8,128)}, f32[8,72,128]{2,1,0:T(8,128)S(1)}, u32[]{:S(2)}) copy-start(f32[8,72,128]{2,1,0:T(8,128)S(1)} %all-to-all-done.1.own_ref) | copy-start | bytes 884740
  43.8 40.8 %collective-permute-start.1 = (f32[8,72,128]{2,1,0:T(8,128)S(1)}, f32[8,72,128]{2,1,0:T(8,128)S(1)}, u32[]{:S(2)}, u32[]{:S(2)}) collective-permute-start(f32[8,72,128]{2,1,0:T(8,128)S(1)} %all-to-all-done.1.own_ref), channel_id=1, source_target_pairs={{0,1},{1,0},{2,3},{3,2},{4,5},{5,4},{6,7},{7,6},{8,9},{9,8},{10,11... | collective-permute-start | bytes 884744 | tf_op jit(solution)/shard_map/ppermute | solution.py:452
  45.1 39.5 %collective-permute-start.3 = (bf16[128,384]{1,0:T(8,128)(2,1)S(1)}, bf16[128,384]{1,0:T(8,128)(2,1)S(1)}, u32[]{:S(2)}, u32[]{:S(2)}) collective-permute-start(bf16[128,384]{1,0:T(8,128)(2,1)S(1)} %pad_maximum_fusion.1), channel_id=1, source_target_pairs={{0,2},{2,4},{4,6},{6,8},{8,10},{10,12},{12,14},{1,3},{3,5},{5,7},{... | collective-permute-start | bytes 294920 | tf_op jit(solution)/shard_map/ppermute | solution.py:444
  48.5 36.2 %collective-permute-start.4 = (bf16[128,384]{1,0:T(8,128)(2,1)S(1)}, bf16[128,384]{1,0:T(8,128)(2,1)S(1)}, u32[]{:S(2)}, u32[]{:S(2)}) collective-permute-start(bf16[128,384]{1,0:T(8,128)(2,1)S(1)} %pad_maximum_fusion.2), channel_id=1, source_target_pairs={{2,0},{4,2},{6,4},{8,6},{10,8},{12,10},{14,12},{3,1},{5,3},{7,5},{... | collective-permute-start | bytes 294920 | tf_op jit(solution)/shard_map/ppermute | solution.py:445
  84.6 0.7 copy-start.6
  84.6 0.8 copy-start.10
  84.6 0.8 copy-start.11
  85.4 29.4 %copy-start.5 = (bf16[27,64,64]{2,1,0:T(8,128)(2,1)S(1)}, bf16[27,64,64]{2,1,0:T(8,128)(2,1)}, u32[]{:S(2)}) copy-start(bf16[27,64,64]{2,1,0:T(8,128)(2,1)} %param.16) | copy-start | bytes 663556
  106.8 1.6 collective-permute-start.5
  110.0 13.6 %all-to-all-start.2 = ((f32[8,56,128]{2,1,0:T(8,128)}), f32[8,56,128]{2,1,0:T(8,128)S(1)}, u32[]{:S(2)}, u32[]{:S(2)}) async-start(f32[8,56,128]{2,1,0:T(8,128)} %bitcast.27), calls=%async_computation.2 | async-start | bytes 458752 | tf_op jit(solution)/shard_map/all_to_all | solution.py:483
  124.3 11.7 %all-to-all-start.3 = ((f32[8,56,128]{2,1,0:T(8,128)}), f32[8,56,128]{2,1,0:T(8,128)S(1)}, u32[]{:S(2)}, u32[]{:S(2)}) async-start(f32[8,56,128]{2,1,0:T(8,128)} %broadcast_in_dim.2), calls=%async_computation.3 | async-start | bytes 458752 | tf_op jit(solution)/shard_map/all_to_all | solution.py:485
  135.9 18.5 %collective-permute-start.6 = (f32[448,128]{1,0:T(8,128)S(1)}, f32[448,128]{1,0:T(8,128)S(1)}, u32[]{:S(2)}, u32[]{:S(2)}) collective-permute-start(f32[448,128]{1,0:T(8,128)S(1)} %bitcast.81), channel_id=1, source_target_pairs={{0,1},{1,0},{2,3},{3,2},{4,5},{5,4},{6,7},{7,6},{8,9},{9,8},{10,11... | collective-permute-start | bytes 688136 | tf_op jit(solution)/shard_map/ppermute | solution.py:486
  154.5 3.1 %copy-start.1 = (bf16[27,64]{1,0:T(8,128)(2,1)S(1)}, bf16[27,64]{1,0:T(8,128)(2,1)}, u32[]{:S(2)}) copy-start(bf16[27,64]{1,0:T(8,128)(2,1)} %param.17) | copy-start | bytes 10372

commit v2 on v1

--- a/solution.py
+++ b/solution.py
@@ -40,7 +40,8 @@
     cos, sin = cos * used[:, None], -sin * used[:, None]
     shape = (half + 128, wide, 2, keep)
     both = np.stack([cos.reshape(shape), sin.reshape(shape)], axis=2)
-    return split_table(both.reshape(half + 128, wide * 4 * keep))
+    table = split_table(both.reshape(half + 128, wide * 4 * keep))
+    return table[:, :half], table[:, half:]
 
 
 def x_table(total):
@@ -64,6 +65,14 @@
 
 def lanes_of(shape):
     return lax.broadcasted_iota(jnp.int32, shape, len(shape) - 1)
+
+
+def on_chip(x):
+    return pltpu.with_memory_space_constraint(x, pltpu.VMEM)
+
+
+def off_chip(x):
+    return pltpu.with_memory_space_constraint(x, pltpu.HBM)
 
 
 def forward_y_kernel(index_ref, own_ref, other_ref, table_ref, out_ref):
@@ -75,8 +84,8 @@
         axis=0,
     )
     high, low = parts_of(stacked)
-    t_high = table_ref[0, :half, :]
-    t_low = table_ref[1, :half, :]
+    t_high = table_ref[0]
+    t_low = table_ref[1]
     total = dot(high, t_high) + dot(low, t_high) + dot(high, t_low)
     lane = lanes_of((1, 128))
     sign = (1 - 2 * (lane % 2)).astype(f32)
@@ -101,9 +110,9 @@
         out_shape=jax.ShapeDtypeStruct((wide, rows, 128), f32),
         in_specs=[pl.BlockSpec(memory_space=pltpu.SMEM)] + [pl.BlockSpec(memory_space=pltpu.VMEM)] * 3,
         out_specs=pl.BlockSpec(memory_space=pltpu.VMEM),
-        compiler_params=pltpu.CompilerParams(vmem_limit_bytes=40 << 20),
+        compiler_params=pltpu.CompilerParams(vmem_limit_bytes=10 << 20),
         name="forward_y",
-    )(index, own, other, table)
+    )(index, own, other, off_chip(table))
 
 
 def along_x_kernel(in_ref, table_ref, weight_ref, out_ref, line_ref):
@@ -127,20 +136,93 @@
     line_ref[8 + total :] = jnp.zeros((8, lanes), f32)
     line_ref[8 : 8 + total] = back[:total] - sign * pltpu.roll(back[total:], 64, 1)
     for w in range(wide):
-        out_ref[w] = line_ref[6 + rows * w : 6 + rows * w + held]
+        out_ref[w] = line_ref[6 + rows * w : 6 + rows * w + held].astype(out_ref.dtype)
 
 
 def along_x(pieces, table, weight_lines):
     wide, rows, lanes = pieces.shape
     return pl.pallas_call(
         along_x_kernel,
-        out_shape=jax.ShapeDtypeStruct((wide, rows + 8, lanes), f32),
+        out_shape=jax.ShapeDtypeStruct((wide, rows + 8, lanes), bf16),
         in_specs=[pl.BlockSpec(memory_space=pltpu.VMEM)] * 3,
         out_specs=pl.BlockSpec(memory_space=pltpu.VMEM),
         scratch_shapes=[pltpu.VMEM((wide * rows + 16, lanes), f32)],
-        compiler_params=pltpu.CompilerParams(vmem_limit_bytes=40 << 20),
+        compiler_params=pltpu.CompilerParams(vmem_limit_bytes=12 << 20),
         name="along_x",
     )(pieces, table, weight_lines)
+
+
+def turn_mid_kernel(
+    index_ref, whole, other, out_hbm, sent_ref, into, side, sems, last_ref, last_sem, out_ref, out_sems
+):
+    channels, slices, rows, half = into.shape
+    narrow = index_ref[0]
+    copies = start_blocks(narrow, whole, other, into, side, sems)
+    block = pl.multiple_of((rows - 16) * (1 - narrow), 16)
+    fetch = pltpu.make_async_copy(other.at[:, :, pl.ds(block, 16), :], last_ref, last_sem)
+    fetch.start()
+    for b, pair in enumerate(copies):
+        for copy in pair:
+            copy.wait()
+        span = slice(16 * b, 16 * b + 16)
+        for z in range(2):
+            out_ref[span, z, :, :half] = jnp.swapaxes(into[:, z, span, :], 0, 1)
+            out_ref[span, z, :, half:] = jnp.swapaxes(side[:, z, span, :], 0, 1)
+        pltpu.make_async_copy(out_ref.at[span], out_hbm.at[span], out_sems.at[b]).start()
+    fetch.wait()
+    for z in range(slices):
+        spot = slice(channels * z, channels * (z + 1))
+        sent_ref[0, spot] = out_ref[(rows - 1) * (1 - narrow), z, :, :half]
+        turned = jnp.swapaxes(last_ref[:, z], 0, 1)
+        sent_ref[1, spot] = jnp.where(
+            narrow == 0, turned[15].astype(f32), turned[0].astype(f32)
+        ).astype(bf16)
+    for b in range(rows // 16):
+        span = slice(16 * b, 16 * b + 16)
+        pltpu.make_async_copy(out_ref.at[span], out_hbm.at[span], out_sems.at[b]).wait()
+
+
+def start_blocks(narrow, whole, other, into, side, sems):
+    tile = pl.ds(pl.multiple_of(128 * narrow, 128), 128)
+    copies = []
+    for b in range(into.shape[2] // 16):
+        span = pl.ds(16 * b, 16)
+        copies.append(
+            (
+                pltpu.make_async_copy(whole.at[:, :, span, :], into.at[:, :, span, :], sems.at[b, 0]),
+                pltpu.make_async_copy(
+                    other.at[:, :, span, tile], side.at[:, :, span, :], sems.at[b, 1]
+                ),
+            )
+        )
+    for pair in copies:
+        for copy in pair:
+            copy.start()
+    return copies
+
+
+def turn_mid(index, value, other):
+    channels, slices, rows, half = value.shape
+    shape = (rows, slices, channels, half + 128)
+    anywhere = pl.BlockSpec(memory_space=pl.ANY)
+    return pl.pallas_call(
+        turn_mid_kernel,
+        out_shape=(pltpu.HBM(shape, bf16), jax.ShapeDtypeStruct((2, 128, half), bf16)),
+        in_specs=[pl.BlockSpec(memory_space=pltpu.SMEM), anywhere, anywhere],
+        out_specs=(anywhere, pl.BlockSpec(memory_space=pltpu.VMEM)),
+        scratch_shapes=[
+            pltpu.VMEM(value.shape, bf16),
+            pltpu.VMEM((channels, slices, rows, 128), bf16),
+            pltpu.SemaphoreType.DMA((rows // 16, 2)),
+            pltpu.VMEM((channels, slices, 16, half), bf16),
+            pltpu.SemaphoreType.DMA,
+            pltpu.VMEM(shape, bf16),
+            pltpu.SemaphoreType.DMA((rows // 16,)),
+        ],
+        compiler_params=pltpu.CompilerParams(vmem_limit_bytes=32 << 20),
+        cost_estimate=pl.CostEstimate(flops=0, bytes_accessed=12 * value.size, transcendentals=0),
+        name="turn_mid",
+    )(index, off_chip(value), off_chip(other))
 
 
 def masked_kernel(
@@ -149,45 +231,56 @@
     own_ref,
     other_ref,
     table_ref,
+    table_side_ref,
     taps_ref,
-    pick_ref,
-    top_ref,
-    bottom_ref,
+    beyond_ref,
+    beside_ref,
+    pick_hbm,
     in_hbm,
+    in_other_hbm,
     mid_hbm,
-    side_hbm,
-    shifted_hbm,
+    masked_hbm,
+    out_ref,
     pay_ref,
     noise_ref,
-    in_ref,
-    mid_ref,
-    side_ref,
-    shifted_ref,
     sum_ref,
     second_ref,
-    sems,
+    in_ref,
+    in_side_ref,
+    in_rows_a,
+    in_rows_b,
+    mid_ref,
+    masked_ref,
+    pick_ref,
+    in_sems,
+    mid_sems,
+    masked_sem,
+    pick_sem,
 ):
     wide, held, lanes = own_ref.shape
     rows = held - 8
-    groups = rows // 8
-    half = mid_ref.shape[1]
+    blocks = rows // 16
+    half = mid_ref.shape[3] - 128
     ext = half + 128
     narrow = index_ref[0]
-    copies = [
-        pltpu.make_async_copy(mid_hbm, mid_ref, sems.at[0]),
-        pltpu.make_async_copy(side_hbm, side_ref, sems.at[1]),
-        pltpu.make_async_copy(in_hbm, in_ref, sems.at[2]),
-    ]
-    for copy in copies:
-        copy.start()
+    copies = []
+    for b in range(blocks):
+        span = slice(16 * b, 16 * b + 16)
+        copies.append(pltpu.make_async_copy(mid_hbm.at[span], mid_ref.at[span], mid_sems.at[b]))
+        copies[b].start()
+    channels = in_ref.shape[0]
+    in_copies = start_blocks(narrow, in_hbm, in_other_hbm, in_ref, in_side_ref, in_sems)
+
+    pick_copy = pltpu.make_async_copy(pick_hbm, pick_ref, pick_sem)
+    pick_copy.start()
 
     lane = lanes_of((1, lanes))
     sign = jnp.where(narrow == 0, 1.0, (1 - 2 * (lane % 2)).astype(f32))
     first = (lane // 32) % 2 == 0
     z_lines = ([], [])
     for w in range(wide):
-        own = own_ref[w] * sign
-        other = other_ref[w] * sign
+        own = own_ref[w].astype(f32) * sign
+        other = other_ref[w].astype(f32) * sign
         even = jnp.where(narrow == 0, own, other)
         odd = jnp.where(narrow == 0, other, own)
         z_lines[0].append(jnp.where(first, even, pltpu.roll(odd, 32, 1)))
@@ -195,8 +288,14 @@
     lines = jnp.concatenate(
         [jnp.concatenate(z_lines[0], axis=1), jnp.concatenate(z_lines[1], axis=1)], axis=0
     )
-    high, low = parts_of(lines)
-    noise = dot_nt(high, table_ref[0]) + dot_nt(low, table_ref[0]) + dot_nt(high, table_ref[1])
+    lines = lines.astype(bf16)
+    noise = jnp.concatenate(
+        [
+            dot_nt(lines, table[0]) + dot_nt(lines, table[1])
+            for table in (table_ref, table_side_ref)
+        ],
+        axis=1,
+    )
     column = lanes_of((1, ext))
     beside = jnp.where(narrow == 0, column - half, ext - 1 - column) < 2
     ours = (column < half) | beside
@@ -206,67 +305,88 @@
         for z in range(2):
             noise_ref[d, z] = moved[z * held : (z + 1) * held]
 
-    copies[0].wait()
-    copies[1].wait()
-    side_ok = lane == jnp.where(narrow == 0, 0, 127)
+    side_lane = jnp.where(narrow == 0, half, ext - 1)
+    kept = (column < half) | (column == side_lane)
 
     def window_of(start):
-        pieces = [noise_ref[d, z, pl.ds(start, 16), :] for z in range(2) for d in range(3)]
-        return jnp.concatenate(pieces + [jnp.zeros((32, ext), f32)], axis=0)
-
-    def store_row(window, tap_row, mask, side, row):
-        value = dot(taps_ref[pl.ds(tap_row * 128, 128), :], window)
-        main = jnp.where(mask.astype(f32) > 0, value[:, :half], 0.0)
-        edge = jnp.where((side.astype(f32) > 0) & side_ok, value[:, half:], 0.0)
-        whole = jnp.concatenate([main, edge], axis=1)
-        where = pl.ds(pl.multiple_of(row * 128, 128), 128)
+        pieces = [noise_ref[d, z, start : start + 16, :] for z in range(2) for d in range(3)]
+        return jnp.concatenate(pieces + [jnp.zeros((32, ext), f32)], axis=0).astype(bf16)
+
+    def store_rows(window, tap_row, mask, row, count):
+        value = dot(taps_ref[tap_row * 128 : (tap_row + count) * 128, :], window)
+        value = jnp.where(mask.astype(f32) > 0, jnp.where(kept, value, 0.0), 0.0)
+        masked_ref[row * 128 : (row + count) * 128, :] = value.astype(bf16)
+
+    for b in range(blocks):
+        copies[b].wait()
+        for h in range(2):
+            window = window_of(16 * b + 8 * h)
+            mid = mid_ref[16 * b + 8 * h : 16 * b + 8 * h + 8].reshape(1024, ext)
+            second = dot_nt(mid[:, :half], window[:, :half])
+            second_ref[...] = second if b == 0 and h == 0 else second_ref[...] + second
+            for m in range(0, 8, 2):
+                store_rows(
+                    window, m + 1, mid[m * 128 : m * 128 + 256], 16 * b + 8 * h + m + 1, 2
+                )
+    for k in range(2):
+        main = jnp.where(narrow == k, beyond_ref[0].astype(f32), beside_ref[1].astype(f32))
+        aside = jnp.where(narrow == k, beyond_ref[1].astype(f32), beside_ref[0].astype(f32))
+        aside = jnp.where(narrow == 0, aside[:, :128], aside[:, half - 128 :])
+        mask = jnp.concatenate([main, aside], axis=1)
+        store_rows(window_of((rows - 8) * k), 9 * k, mask, (rows + 1) * k, 1)
+    keep = pltpu.make_async_copy(masked_ref, masked_hbm, masked_sem)
+    keep.start()
+
+    amount = jnp.where(narrow == 0, 127, 1)
+
+    def turn_in(b, into):
+        for copy in in_copies[b]:
+            copy.wait()
+        span = slice(16 * b, 16 * b + 16)
+        for z in range(2):
+            turned = jnp.swapaxes(in_ref[:, z, span, :], 0, 1)
+            into[1, :, z] = turned
+            flat = turned.reshape(16 * channels, half).astype(f32)
+            beside = jnp.swapaxes(in_side_ref[:, z, span, :], 0, 1)
+            beside = pltpu.roll(beside.reshape(16 * channels, 128).astype(f32), amount, 1)
+            left = flat[:, :128]
+            right = flat[:, 128:]
+            down_left = pltpu.roll(left, 1, 1)
+            down_right = pltpu.roll(right, 1, 1)
+            up_left = pltpu.roll(left, 127, 1)
+            up_right = pltpu.roll(right, 127, 1)
+            from_before = jnp.where(narrow == 0, 0.0, beside)
+            from_after = jnp.where(narrow == 0, beside, 0.0)
+            moved = {
+                (0, 0): jnp.where(lane == 0, from_before, down_left),
+                (0, 1): jnp.where(lane == 0, down_left, down_right),
+                (2, 0): jnp.where(lane == 127, up_right, up_left),
+                (2, 1): jnp.where(lane == 127, from_after, up_right),
+            }
+            for (d, t), value in moved.items():
+                into[d, :, z, :, 128 * t : 128 * t + 128] = value.astype(bf16).reshape(
+                    16, channels, 128
+                )
+
+    in_rows = (in_rows_a, in_rows_b)
+    turn_in(0, in_rows[0])
+    for b in range(blocks):
+        if b + 1 < blocks:
+            turn_in(b + 1, in_rows[(b + 1) % 2])
+        held_rows = in_rows[b % 2]
+        left = jnp.concatenate(
+            [
+                masked_ref[(16 * b + 2 * q) * 128 : (16 * b + 2 * q + 4) * 128, :half]
+                for q in range(8)
+            ],
+            axis=1,
+        )
         for d in range(3):
-            moved = whole if d == 1 else pltpu.roll(whole, (d - 1) % ext, 1)
-            shifted_ref[d, where, :] = moved[:, :half].astype(bf16)
-
-    second_ref[...] = jnp.zeros_like(second_ref)
-
-    def group_body(g, carry):
-        start = pl.multiple_of(g * 8, 8)
-        wide_window = window_of(start)
-        window = wide_window.astype(bf16)
-        turned = wide_window[:, :half].T.astype(bf16)
-        here = pl.ds(pl.multiple_of(g * 1024, 1024), 1024)
-        second_ref[...] += dot(mid_ref[here, :], turned)
-        for m in range(8):
-            spot = pl.ds(pl.multiple_of(g * 1024 + m * 128, 128), 128)
-            store_row(window, m + 1, mid_ref[spot, :], side_ref[spot, :], g * 8 + m + 1)
-        return carry
-
-    lax.fori_loop(0, groups, group_body, 0)
-    window = window_of(0).astype(bf16)
-    store_row(window, 0, top_ref[:, :half], top_ref[:, half:], 0)
-    window = window_of(rows - 8).astype(bf16)
-    store_row(window, 9, bottom_ref[:, :half], bottom_ref[:, half:], rows + 1)
-    outs = [
-        pltpu.make_async_copy(shifted_ref.at[d], shifted_hbm.at[d], sems.at[3 + d])
-        for d in range(3)
-    ]
-    for copy in outs:
-        copy.start()
-
-    copies[2].wait()
-    sum_ref[...] = jnp.zeros_like(sum_ref)
-
-    def chunk_body(k, carry):
-        right = in_ref[pl.ds(pl.multiple_of(k * 4 * half, 4 * half), 4 * half), :]
-        for d in range(3):
-            left = jnp.concatenate(
-                [
-                    shifted_ref[d, pl.ds(pl.multiple_of(k * 1024 + 256 * q, 256), 512), :]
-                    for q in range(4)
-                ],
-                axis=1,
+            right = jnp.concatenate(
+                [held_rows[d, 2 * q : 2 * q + 2].reshape(256, half) for q in range(8)], axis=1
             )
-            sum_ref[d] += dot(left, right)
-        return carry
-
-    lax.fori_loop(0, groups, chunk_body, 0)
+            part = dot_nt(left, right)
+            sum_ref[d] = part if b == 0 else sum_ref[d] + part
 
     singles = []
     for d in range(3):
@@ -285,110 +405,218 @@
     pieces = [
         second_ref[(m * 2 + z) * 64 : (m * 2 + z + 1) * 64, :] for m in range(8) for z in range(2)
     ]
+    pick_copy.wait()
     second = jnp.dot(
-        jnp.concatenate(pieces, axis=1), pick_ref[...], preferred_element_type=f32, precision=highest
+        jnp.concatenate(pieces, axis=1), pick_ref[...].astype(f32), preferred_element_type=f32, precision=highest
     )
     singles.append(second)
     for k in range(5):
         pay_ref[(9 + k) * 64 : (10 + k) * 64] = jnp.where(
             lane < 64, singles[2 * k], pltpu.roll(singles[2 * k + 1], 64, 1)
         )
-    for copy in outs:
-        copy.wait()
-
-
-def masked_and_kernels(index, own, other, table, taps, pick, top, bottom, lines_in, mid, side, scale):
+    out_ref[...] = pay_ref[...].astype(bf16)
+    keep.wait()
+
+
+def masked_and_kernels(
+    index,
+    own,
+    other,
+    table,
+    table_side,
+    taps,
+    pick,
+    beyond,
+    beyond_other,
+    act_in,
+    in_other,
+    rows_mid,
+    scale,
+):
     wide, held, lanes = own.shape
-    rows = held - 8
-    half = mid.shape[1]
-    ext = half + 128
+    rows, slices, channels, ext = rows_mid.shape
     vmem = pl.BlockSpec(memory_space=pltpu.VMEM)
     anywhere = pl.BlockSpec(memory_space=pl.ANY)
     return pl.pallas_call(
         functools.partial(masked_kernel, scale),
         out_shape=(
-            jax.ShapeDtypeStruct((3, (rows + 2) * 128, half), bf16),
-            jax.ShapeDtypeStruct((14 * 64, 128), f32),
+            pltpu.HBM(((rows + 2) * 128, ext), bf16),
+            jax.ShapeDtypeStruct((14 * 64, 128), bf16),
         ),
-        in_specs=[pl.BlockSpec(memory_space=pltpu.SMEM)] + [vmem] * 7 + [anywhere] * 3,
+        in_specs=[pl.BlockSpec(memory_space=pltpu.SMEM)] + [vmem] * 7 + [anywhere] * 4,
         out_specs=(anywhere, vmem),
         scratch_shapes=[
+            pltpu.VMEM((14 * 64, 128), f32),
             pltpu.VMEM((3, 2, held, ext), f32),
-            pltpu.VMEM(lines_in.shape, bf16),
-            pltpu.VMEM(mid.shape, bf16),
-            pltpu.VMEM(side.shape, bf16),
-            pltpu.VMEM((3, (rows + 2) * 128, half), bf16),
             pltpu.VMEM((3, 512, 256), f32),
             pltpu.VMEM((1024, 128), f32),
-            pltpu.SemaphoreType.DMA((6,)),
+            pltpu.VMEM(act_in.shape, bf16),
+            pltpu.VMEM((channels, slices, rows, 128), bf16),
+            pltpu.VMEM((3, 16, slices, channels, ext - 128), bf16),
+            pltpu.VMEM((3, 16, slices, channels, ext - 128), bf16),
+            pltpu.VMEM(rows_mid.shape, bf16),
+            pltpu.VMEM(((rows + 2) * 128, ext), bf16),
+            pltpu.VMEM(pick.shape, bf16),
+            pltpu.SemaphoreType.DMA((rows // 16, 2)),
+            pltpu.SemaphoreType.DMA((rows // 16,)),
+            pltpu.SemaphoreType.DMA,
+            pltpu.SemaphoreType.DMA,
         ],
-        compiler_params=pltpu.CompilerParams(vmem_limit_bytes=56 << 20),
+        compiler_params=pltpu.CompilerParams(vmem_limit_bytes=48 << 20),
         name="masked_and_kernels",
-    )(index, own, other, table, taps, pick, top, bottom, lines_in, mid, side)
-
-
-def input_kernel(shifted_hbm, weight_ref, out_hbm, shifted_ref, out_ref, in_sems, out_sems):
-    rows = out_ref.shape[0] // 128
-    groups = rows // 8
-    chunk = 8 * 128
-    copies = []
-    for g in range(groups):
-        first = 0 if g == 0 else chunk * g + 256
-        last = chunk * (g + 1) + 256
-        copies.append(
-            [
-                pltpu.make_async_copy(
-                    shifted_hbm.at[d, first:last], shifted_ref.at[d, first:last], in_sems.at[g, d]
-                )
-                for d in range(3)
-            ]
+    )(
+        index,
+        own,
+        other,
+        off_chip(table),
+        off_chip(table_side),
+        taps,
+        beyond,
+        beyond_other,
+        off_chip(pick),
+        off_chip(act_in),
+        off_chip(in_other),
+        off_chip(rows_mid),
+    )
+
+
+def arrange_kernel(taps_ref, weight_ref):
+    for dy in range(3):
+        for par, i4 in ((0, 3), (1, 0)):
+            weight_ref[
+                par * 128 : (par + 1) * 128, dy * 512 + i4 * 128 : dy * 512 + (i4 + 1) * 128
+            ] = jnp.zeros((128, 128), bf16)
+        for dx in range(3):
+            for z in range(2):
+                tap = dx * 3 + dy
+                tile = jnp.concatenate([taps_ref[(z + 1) * 9 + tap], taps_ref[z * 9 + tap]], axis=1)
+                for par in range(2):
+                    spot = dy * 512 + (par + 2 - dx) * 128
+                    weight_ref[
+                        par * 128 + z * 64 : par * 128 + (z + 1) * 64, spot : spot + 128
+                    ] = tile
+
+
+def arrange(w_first):
+    vmem = pl.BlockSpec(memory_space=pltpu.VMEM)
+    return pl.pallas_call(
+        arrange_kernel,
+        out_shape=jax.ShapeDtypeStruct((256, 1536), bf16),
+        in_specs=[vmem],
+        out_specs=vmem,
+        name="arrange",
+    )(w_first)
+
+
+def input_kernel(base, masked_hbm, weight_ref, *rest):
+    out_hbm, masked_ref, shifted_ref, wide_ref, out_ref, in_sems, out_sems = rest[-7:]
+    rows = shifted_ref.shape[1] // 128 - 2
+    fetches = []
+    for step in range(rows // 8):
+        first = 0 if step == 0 else (8 * step + 2) * 128
+        last = (8 * step + 10) * 128
+        fetches.append(
+            pltpu.make_async_copy(
+                masked_hbm.at[base * 128 + first : base * 128 + last],
+                masked_ref.at[first:last],
+                in_sems.at[step],
+            )
         )
-    for group in copies:
-        for copy in group:
+        fetches[step].start()
+    ext = masked_ref.shape[1]
+    half = ext - 128
+    channels = out_ref.shape[1]
+    def shift(row):
+        spot = slice(row * 128, (row + 1) * 128)
+        whole = masked_ref[spot, :]
+        shifted_ref[1, spot, :] = whole[:, :half]
+        whole = whole.astype(f32)
+        for d in (0, 2):
+            shifted_ref[d, spot, :] = pltpu.roll(whole, (d - 1) % ext, 1)[:, :half].astype(bf16)
+
+    ready = 0
+    outs = []
+    for step in range(rows // 8):
+        fetches[step].wait()
+        while ready < 8 * step + 10:
+            shift(ready)
+            ready += 1
+        for q in range(4):
+            row = (8 * step + 2 * q) * 128
+            stacked = jnp.concatenate(
+                [shifted_ref[d, row : row + 512, :] for d in range(3)], axis=0
+            )
+            value = dot(weight_ref[...], stacked).astype(bf16)
+            wide_ref[step % 4, 2 * q * 128 : (2 * q + 2) * 128, :] = value
+        if step % 2 == 1:
+            block = step // 2
+            pair = jnp.concatenate([wide_ref[(step - 1) % 4], wide_ref[step % 4]], axis=0)
+            pair = pair.reshape(16, 2, channels, half)
+            for z in range(2):
+                out_ref[block, :, z] = jnp.swapaxes(pair[:, z], 0, 1)
+            first = base + 16 * block
+            copy = pltpu.make_async_copy(
+                out_ref.at[block], out_hbm.at[:, :, first : first + 16, :], out_sems.at[block]
+            )
             copy.start()
-    outs = []
-    for g in range(groups):
-        for copy in copies[g]:
-            copy.wait()
-
-        def pair(q, carry, g=g):
-            row = pl.multiple_of(g * chunk + q * 256, 256)
-            stacked = jnp.concatenate(
-                [shifted_ref[d, pl.ds(row, 512), :] for d in range(3)], axis=0
-            )
-            out_ref[pl.ds(row, 256), :] = dot(weight_ref[...], stacked).astype(bf16)
-            return carry
-
-        lax.fori_loop(0, 4, pair, 0)
-        span = slice(g * chunk, (g + 1) * chunk)
-        copy = pltpu.make_async_copy(out_ref.at[span], out_hbm.at[span], out_sems.at[g])
-        copy.start()
-        outs.append(copy)
+            outs.append(copy)
     for copy in outs:
         copy.wait()
 
 
-def input_gradient(shifted, weight):
-    taps, count, half = shifted.shape
-    rows = count // 128 - 2
+def input_gradient(masked, weight, base, rows, shape, earlier=None):
+    ext = masked.shape[1]
+    half = ext - 128
+    channels = shape[0]
     anywhere = pl.BlockSpec(memory_space=pl.ANY)
+    extra = () if earlier is None else (earlier,)
     return pl.pallas_call(
-        input_kernel,
-        out_shape=jax.ShapeDtypeStruct((rows * 128, half), bf16),
-        in_specs=[anywhere, pl.BlockSpec(memory_space=pltpu.VMEM)],
+        functools.partial(input_kernel, base),
+        out_shape=jax.ShapeDtypeStruct(shape, bf16),
+        in_specs=[anywhere, pl.BlockSpec(memory_space=pltpu.VMEM)] + [anywhere] * len(extra),
         out_specs=anywhere,
         scratch_shapes=[
-            pltpu.VMEM(shifted.shape, bf16),
-            pltpu.VMEM((rows * 128, half), bf16),
-            pltpu.SemaphoreType.DMA((rows // 8, 3)),
+            pltpu.VMEM(((rows + 2) * 128, ext), bf16),
+            pltpu.VMEM((3, (rows + 2) * 128, half), bf16),
+            pltpu.VMEM((4, 1024, half), bf16),
+            pltpu.VMEM((rows // 16, channels, 2, 16, half), bf16),
             pltpu.SemaphoreType.DMA((rows // 8,)),
+            pltpu.SemaphoreType.DMA((rows // 16,)),
         ],
+        input_output_aliases={} if earlier is None else {2: 0},
         cost_estimate=pl.CostEstimate(
             flops=2 * rows * 128 * half * 1536, bytes_accessed=4 * rows * 128 * half * 2, transcendentals=0
         ),
-        compiler_params=pltpu.CompilerParams(vmem_limit_bytes=40 << 20),
+        compiler_params=pltpu.CompilerParams(vmem_limit_bytes=30 << 20),
         name="input_gradient",
-    )(shifted, weight)
+    )(off_chip(masked), weight, *extra)
+
+
+def unpack_kernel(pay_ref, first_ref, second_ref):
+    slots = [pay_ref[64 * k : 64 * k + 64].astype(f32) for k in range(14)]
+    for slot in range(9):
+        tap = slot % 3 * 3 + slot // 3
+        first_ref[18 + tap] = slots[slot][:, :64]
+        first_ref[tap] = pltpu.roll(slots[slot], 64, 1)[:, :64]
+        single = slots[9 + slot // 2]
+        if slot % 2 == 1:
+            single = pltpu.roll(single, 64, 1)
+        first_ref[9 + tap] = single[:, :64]
+    second_ref[...] = pltpu.roll(slots[13], 64, 1).T[:27]
+
+
+def unpack(pay):
+    vmem = pl.BlockSpec(memory_space=pltpu.VMEM)
+    return pl.pallas_call(
+        unpack_kernel,
+        out_shape=(
+            jax.ShapeDtypeStruct((27, 64, 64), f32),
+            jax.ShapeDtypeStruct((27, 64), f32),
+        ),
+        in_specs=[vmem],
+        out_specs=(vmem, vmem),
+        name="unpack",
+    )(on_chip(pay))
 
 
 def tap_choice():
@@ -405,18 +633,6 @@
     return choice
 
 
-def kernel_matrix(w_first):
-    channels = w_first.shape[1]
-    w = w_first.reshape(3, 3, 3, channels, channels)
-    grid = jnp.stack([jnp.stack([w[1], w[0]]), jnp.stack([w[2], w[1]])])
-    grid = grid.transpose(2, 3, 0, 4, 1, 5).reshape(3, 3, 128, 128)
-    none = jnp.zeros((3, 128, 128), w.dtype)
-    row0 = jnp.stack([grid[2], grid[1], grid[0], none], axis=2)
-    row1 = jnp.stack([none, grid[2], grid[1], grid[0]], axis=2)
-    both = jnp.stack([row0, row1])
-    return both.transpose(0, 2, 1, 3, 4).reshape(256, 1536)
-
-
 def fast(denoised, clean_volume, weight, act_in, act_mid, w_first, w_second):
     wide = lax.axis_size("wide")
     slices, rows, half = denoised.shape
@@ -424,76 +640,75 @@
     keep = weight.shape[0]
     total_x = wide * rows
     total_y = 2 * half
+    ext = half + 128
     narrow = lax.axis_index("narrow")
     index = narrow.astype(jnp.int32).reshape(1)
     swap = [(0, 1), (1, 0)]
-    table_y = jnp.asarray(y_table(wide, keep, half))
+    up = [(i, i + 1) for i in range(wide - 1)]
+    down = [(j, i) for i, j in up]
+    table_y, table_side = (jnp.asarray(t) for t in y_table(wide, keep, half))
     table_x = jnp.asarray(x_table(total_x))
+    choice = tap_choice()
+    pick = np.zeros((16 * 128, 128), np.float32)
+    pick[:, :27] = choice[:, 1:9].reshape(27, 16 * 128).T
 
     error = denoised - clean_volume
     error_other = lax.ppermute(error, "narrow", swap)
+    act_mid, act_in, error_other = lax.optimization_barrier((act_mid, act_in, error_other))
+    mid_other = lax.ppermute(act_mid, "narrow", swap)
+    in_other = lax.ppermute(act_in, "narrow", swap)
     lines = forward_y(index, error, error_other, table_y, wide)
+
+    lines, act_mid, weight = lax.optimization_barrier((lines, act_mid, weight))
     lines = lax.all_to_all(lines, "wide", 0, 0, tiled=True)
-
-    mid = act_mid.transpose(2, 1, 0, 3).reshape(rows * 128, half)
-    edge = jnp.where(narrow == 0, act_mid[..., half - 128 :], act_mid[..., :128])
-    side = lax.ppermute(edge, "narrow", swap).transpose(2, 1, 0, 3).reshape(rows * 128, 128)
-    first = jnp.concatenate([mid[:128], side[:128]], axis=1)
-    last = jnp.concatenate([mid[-128:], side[-128:]], axis=1)
-    up = [(i, i + 1) for i in range(wide - 1)]
-    top = lax.ppermute(last, "wide", up)
-    bottom = lax.ppermute(first, "wide", [(j, i) for i, j in up])
-    lines_in = act_in.reshape(channels, slices, rows // 2, 2, half)
-    lines_in = lines_in.transpose(2, 4, 3, 1, 0).reshape(rows // 2 * half, 256)
-
+    rows_mid, sent = turn_mid(index, act_mid, mid_other)
+    ways = [(2 * i, 2 * j) for i, j in up] + [(2 * i + 1, 2 * j + 1) for i, j in down]
+    beyond = lax.ppermute(sent, ("wide", "narrow"), ways)
     weight_lines = jnp.tile(weight.T, (1, 4))
+    lines, weight_lines = lax.optimization_barrier((lines, weight_lines))
     lines = along_x(lines, table_x, weight_lines)
+
+    lines, beyond, w_first, w_second = lax.optimization_barrier((lines, beyond, w_first, w_second))
     lines = lax.all_to_all(lines, "wide", 0, 0, tiled=True)
-    lines_other = lax.ppermute(lines, "narrow", swap)
-
-    choice = tap_choice()
+    beyond_other = lax.ppermute(beyond, "narrow", swap)
+    matrix = arrange(w_first)
     taps = jnp.einsum(
         "tc,tmzk->mzck", w_second, jnp.asarray(choice, bf16), preferred_element_type=f32
     )
     taps = taps.astype(bf16).reshape(1280, 128)
-    pick = np.zeros((16 * 128, 128), np.float32)
-    pick[:, :27] = choice[:, 1:9].reshape(27, 16 * 128).T
-    shifted, pay = masked_and_kernels(
+    lines, matrix, taps, beyond_other = lax.optimization_barrier(
+        (lines, matrix, taps, beyond_other)
+    )
+    lines_other = lax.ppermute(lines, "narrow", swap)
+    masked, pay = masked_and_kernels(
         index,
         lines,
         lines_other,
         table_y,
+        table_side,
         taps,
-        jnp.asarray(pick),
-        top,
-        bottom,
-        lines_in,
-        mid,
-        side,
+        jnp.asarray(pick, bf16),
+        beyond,
+        beyond_other,
+        act_in,
+        in_other,
+        rows_mid,
         -2.0 / (total_x * total_y),
     )
-    grad_in = input_gradient(shifted, kernel_matrix(w_first))
-    grad_in = grad_in.reshape(rows, slices, channels, half).transpose(2, 1, 0, 3)
-
-    count = pay.shape[0] // 2
-    mine = lax.dynamic_slice_in_dim(pay, narrow * count, count, 0)
-    theirs = lax.dynamic_slice_in_dim(pay, (1 - narrow) * count, count, 0)
-    mine = mine + lax.ppermute(theirs, "narrow", swap)
-    mine = mine.reshape(wide, count // wide, 128)
-    mine = lax.all_to_all(mine, "wide", 0, 0, tiled=True)
-    mine = jnp.broadcast_to(mine.sum(axis=0, keepdims=True), mine.shape)
-    mine = lax.all_to_all(mine, "wide", 0, 0, tiled=True).reshape(count, 128)
-    theirs = lax.ppermute(mine, "narrow", swap)
-    pay = jnp.concatenate(
-        [jnp.where(narrow == 0, mine, theirs), jnp.where(narrow == 0, theirs, mine)], axis=0
-    )
-    pay = pay.reshape(14, 64, 2, 64)
-    outer = pay[:9].reshape(3, 3, 64, 2, 64)
-    inner = pay[9:].transpose(0, 2, 1, 3).reshape(10, 64, 64)
-    grad_second = inner[9, :, :27].T
-    inner = inner[:9].reshape(3, 3, 64, 64)
-    grad_first = jnp.stack([outer[:, :, :, 1], inner, outer[:, :, :, 0]])
-    grad_first = grad_first.transpose(0, 2, 1, 3, 4).reshape(27, channels, channels)
+
+    pay = pay.reshape(wide, pay.shape[0] // wide, 128)
+    pay, matrix = lax.optimization_barrier((pay, matrix))
+    pay = lax.all_to_all(pay, "wide", 0, 0, tiled=True)
+    grad_in = input_gradient(masked, matrix, 0, rows // 2, act_in.shape)
+    pay, grad_in = lax.optimization_barrier((pay, grad_in))
+    total = pay.astype(f32).sum(axis=0)
+    total = total + lax.ppermute(total, "narrow", swap)
+    pay = jnp.broadcast_to(total.astype(bf16)[None], pay.shape)
+    pay, grad_in, matrix = lax.optimization_barrier((pay, grad_in, matrix))
+    pay = lax.all_to_all(pay, "wide", 0, 0, tiled=True)
+    grad_in = input_gradient(masked, matrix, rows // 2, rows // 2, act_in.shape, grad_in)
+    pay, grad_in = lax.optimization_barrier((pay, grad_in))
+    grad_first, grad_second = unpack(pay.reshape(-1, 128))
     return (grad_in, grad_first, grad_second)
 
 

time: 159 us -> 89.9 us (0.57)
  local copies, waits for them, and re-layouts: 50.6 us -> 0.89 us
  waiting for transfers between devices: 34.3 us -> 13.5 us
  Pallas kernels: 38.1 us -> 47.5 us
  other arithmetic: 8.38 us -> 1.03 us
    reshape x6 -> x0, local copies, waits for them, and re-layouts: 21.8 us -> none  [the longest x2 10.3 us: fast(): lines_in = act_in.reshape(channels, slices, rows // 2, 2, half)]
    transpose x6 -> x0, local copies, waits for them, and re-layouts: 12.5 us -> none  [the longest x1 6.55 us: fast(): mid = act_mid.transpose(2, 1, 0, 3).reshape(rows * 128, half)]
    all_to_all x2, waiting for transfers between devices: 17.5 us -> 5.1 us  [fast(): lines = lax.all_to_all(lines, 'wide', 0, 0, tiled=True)]
    unnamed x28 -> x10, local copies, waits for them, and re-layouts: 9.38 us -> 0.03 us
    pallas_call x2 -> x6, Pallas kernels: 34.5 us -> 42.7 us  [the longest x1 20.5 us: masked_and_kernels(): pl.pallas_call(functools.partial(masked_kernel, scale), out_shape=(pltpu....]
    all_to_all x2, waiting for transfers between devices: 11.7 us -> 3.79 us  [fast(): pay = lax.all_to_all(pay, 'wide', 0, 0, tiled=True)]
    slice x15 -> x0, local copies, waits for them, and re-layouts: 4.78 us -> none  [the longest x4 2.68 us: fast(): first = jnp.concatenate([mid[:128], side[:128]], axis=1)]
    select_n x2 -> x0, other arithmetic: 3.92 us -> none  [the longest x1 3.89 us: fast(): edge = jnp.where(narrow == 0, act_mid[..., half - 128:], act_mid[..., :128])]
  transfers between devices with their start and end apart: 11 -> 11, of which waited for: 6 -> 7; matrix products, arithmetic and copies ran while one was open for 30% -> 0% of each run, Pallas kernels for 11% -> 29%
where the time goes in v2:
time: 89.9 us; the launch traced here: 89.3 us
  Pallas kernels  47.5 us (53%)
  starting transfers between devices  25.2 us (28%)
  waiting for transfers between devices  13.5 us (15%)
  other arithmetic  1.03 us (1%)
    pallas_call x1, Pallas kernels, masked_and_kernels(): pl.pallas_call(functools.partial(masked_kernel, scale), out_shape=(pltpu....  20.5 us
    pallas_call x2, Pallas kernels, input_gradient(): pl.pallas_call(functools.partial(input_kernel, base), out_shape=jax.Shape...  13.9 us
    all_to_all x2, starting transfers between devices, fast(): lines = lax.all_to_all(lines, 'wide', 0, 0, tiled=True)  12.7 us
    all_to_all x2, starting transfers between devices, fast(): pay = lax.all_to_all(pay, 'wide', 0, 0, tiled=True)  7.36 us
    pallas_call x1, Pallas kernels, turn_mid(): pl.pallas_call(turn_mid_kernel, out_shape=(pltpu.HBM(shape, bf16), jax.Sh...  5.22 us
    all_to_all x2, waiting for transfers between devices, fast(): lines = lax.all_to_all(lines, 'wide', 0, 0, tiled=True)  5.1 us
    ppermute x1, starting transfers between devices, fast(): beyond = lax.ppermute(sent, ('wide', 'narrow'), ways)  4.07 us
    all_to_all x2, waiting for transfers between devices, fast(): pay = lax.all_to_all(pay, 'wide', 0, 0, tiled=True)  3.79 us
  transfers between devices with their start and end apart: 11, of which 7 were waited for; matrix products, arithmetic and copies ran while one was open for 0% of the time, Pallas kernels for 29%

profile of v2, /device:TPU:0, one launch (start us, length us, event | category | flops | bytes accessed | tf_op | source)
XLA Modules:
  0.0 89.3 jit_solution(15212425336486029475)
XLA Ops:
  0.6 1.0 %sub.3.own_ref = f32[2,64,256]{2,1,0:T(8,128)S(1)} subtract(f32[2,64,256]{2,1,0:T(8,128)} %param.12, f32[2,64,256]{2,1,0:T(8,128)} %param.13) | non-fusion elementwise | flops 32768 | bytes 393216 | tf_op jit(solution)/shard_map/sub | solution.py:655
  1.6 0.5 collective-permute-start
  2.2 1.0 %collective-permute-done.other_ref = f32[2,64,256]{2,1,0:T(8,128)S(1)} collective-permute-done((f32[2,64,256]{2,1,0:T(8,128)S(1)}, f32[2,64,256]{2,1,0:T(8,128)S(1)}, u32[]{:S(2)}, u32[]{:S(2)}) %collective-permute-start) | collective-permute-done | bytes 131104 | tf_op jit(solution)/shard_map/ppermute | solution.py:656
  3.1 0.4 collective-permute-start.1
  3.7 2.6 %forward_y.1 = f32[8,64,128]{2,1,0:T(8,128)} custom-call(s32[1]{0:T(128)} %bitcast.index_ref, f32[2,64,256]{2,1,0:T(8,128)S(1)} %sub.3.own_ref, f32[2,64,256]{2,1,0:T(8,128)S(1)} %collective-permute-done.other_ref, bf16[2,256,1024]{2,1,0:T(8,128)(2,1)} %constant.16.clone.table_ref), custom_call_target="tpu_custom_call" | custom-call | tf_op jit(solution)/shard_map/forward_y/pallas_call | solution.py:108
  6.3 7.2 %all-to-all-start = ((f32[8,64,128]{2,1,0:T(8,128)}), f32[8,64,128]{2,1,0:T(8,128)S(1)}, u32[]{:S(2)}, u32[]{:S(2)}) async-start(f32[8,64,128]{2,1,0:T(8,128)} %forward_y.1), calls=%async_computation | async-start | bytes 524288 | tf_op jit(solution)/shard_map/all_to_all | solution.py:663
  13.5 5.2 %turn_mid.1 = (bf16[64,2,64,384]{3,2,1,0:T(8,128)(2,1)}, bf16[2,128,256]{2,1,0:T(8,128)(2,1)S(1)}) custom-call(s32[1]{0:T(128)} %bitcast.index_ref, bf16[64,2,64,256]{3,2,1,0:T(8,128)(2,1)} %whole, bf16[64,2,64,256]{3,2,1,0:T(8,128)(2,1)} %collective-permute-done.1.other), custom_call_target="tpu_custom_call" | custom-call | bytes 25165824 | tf_op jit(solution)/shard_map/turn_mid/pallas_call | solution.py:208
  18.7 4.1 %collective-permute-start.2 = (bf16[2,128,256]{2,1,0:T(8,128)(2,1)S(1)}, bf16[2,128,256]{2,1,0:T(8,128)(2,1)S(1)}, u32[]{:S(2)}, u32[]{:S(2)}) collective-permute-start(bf16[2,128,256]{2,1,0:T(8,128)(2,1)S(1)} %get-tuple-element.41), channel_id=1, source_target_pairs={{0,2},{2,4},{4,6},{6,8},{8,10},{10,12},{12,14},{3,1},{5,3},{7,5},{... | collective-permute-start | bytes 393224 | tf_op jit(solution)/shard_map/ppermute | solution.py:666
  23.0 2.2 %along_x.1 = bf16[8,72,128]{2,1,0:T(8,128)(2,1)} custom-call(f32[8,64,128]{2,1,0:T(8,128)S(1)} %all-to-all-done.in_ref, bf16[2,1024,512]{2,1,0:T(8,128)(2,1)S(1)} %copy-done.2, f32[512,128]{1,0:T(8,128)S(1)} %copy.17.weight_ref), custom_call_target="tpu_custom_call" | custom-call | tf_op jit(solution)/shard_map/along_x/pallas_call | solution.py:144
  25.1 1.0 %collective-permute-done.2.beyond_ref = bf16[2,128,256]{2,1,0:T(8,128)(2,1)S(1)} collective-permute-done((bf16[2,128,256]{2,1,0:T(8,128)(2,1)S(1)}, bf16[2,128,256]{2,1,0:T(8,128)(2,1)S(1)}, u32[]{:S(2)}, u32[]{:S(2)}) %collective-permute-start.2) | collective-permute-done | bytes 131104 | tf_op jit(solution)/shard_map/ppermute | solution.py:666
  26.1 5.6 %all-to-all-start.1 = ((bf16[8,72,128]{2,1,0:T(8,128)(2,1)}), bf16[8,72,128]{2,1,0:T(8,128)(2,1)S(1)}, u32[]{:S(2)}, u32[]{:S(2)}) async-start(bf16[8,72,128]{2,1,0:T(8,128)(2,1)} %along_x.1), calls=%async_computation.1 | async-start | bytes 294912 | tf_op jit(solution)/shard_map/all_to_all | solution.py:672
  31.7 2.0 %arrange.1.weight_ref = bf16[256,1536]{1,0:T(8,128)(2,1)} custom-call(bf16[27,64,64]{2,1,0:T(8,128)(2,1)} %taps_ref), custom_call_target="tpu_custom_call" | custom-call | tf_op jit(solution)/shard_map/arrange/pallas_call | solution.py:502
  34.1 5.1 %all-to-all-done.1.own_ref = bf16[8,72,128]{2,1,0:T(8,128)(2,1)S(1)} async-done(((bf16[8,72,128]{2,1,0:T(8,128)(2,1)}), bf16[8,72,128]{2,1,0:T(8,128)(2,1)S(1)}, u32[]{:S(2)}, u32[]{:S(2)}) %all-to-all-start.1) | async-done | bytes 147488 | tf_op jit(solution)/shard_map/all_to_all | solution.py:672
  39.2 1.4 %collective-permute-done.4.other_ref = bf16[8,72,128]{2,1,0:T(8,128)(2,1)S(1)} collective-permute-done((bf16[8,72,128]{2,1,0:T(8,128)(2,1)S(1)}, bf16[8,72,128]{2,1,0:T(8,128)(2,1)S(1)}, u32[]{:S(2)}, u32[]{:S(2)}) %collective-permute-start.4) | collective-permute-done | bytes 147488 | tf_op jit(solution)/shard_map/ppermute | solution.py:682
  40.5 20.5 %masked_and_kernels.1 = (bf16[8448,384]{1,0:T(8,128)(2,1)}, bf16[896,128]{1,0:T(8,128)(2,1)}) custom-call(s32[1]{0:T(128)} %bitcast.index_ref, bf16[8,72,128]{2,1,0:T(8,128)(2,1)S(1)} %all-to-all-done.1.own_ref, bf16[8,72,128]{2,1,0:T(8,128)(2,1)S(1)} %collective-permute-done.4.other_ref, bf16[2,256,1024]{2,1,0:T(8,128)(2,1)} %constant.16.clone.table_ref, ...), custom_call_target="tpu_custom_call" | custom-call | tf_op jit(solution)/shard_map/masked_and_kernels/pallas_call | solution.py:440
  61.0 3.4 %all-to-all-start.2 = ((bf16[8,112,128]{2,1,0:T(8,128)(2,1)}), bf16[8,112,128]{2,1,0:T(8,128)(2,1)S(1)}, u32[]{:S(2)}, u32[]{:S(2)}) async-start(bf16[8,112,128]{2,1,0:T(8,128)(2,1)} %bitcast.7), calls=%async_computation.2 | async-start | bytes 458752 | tf_op jit(solution)/shard_map/all_to_all | solution.py:701
  64.5 6.9 %input_gradient.2.rest_0_ = bf16[64,2,64,256]{3,2,1,0:T(8,128)(2,1)} custom-call(bf16[8448,384]{1,0:T(8,128)(2,1)} %get-tuple-element.54.masked_hbm, bf16[256,1536]{1,0:T(8,128)(2,1)S(1)} %copy-done.1), custom_call_target="tpu_custom_call" | custom-call | flops 3221225472 | bytes 8388608 | tf_op jit(solution)/shard_map/input_gradient/pallas_call | solution.py:573
  71.4 2.0 %all-to-all-done.2 = bf16[8,112,128]{2,1,0:T(8,128)(2,1)S(1)} async-done(((bf16[8,112,128]{2,1,0:T(8,128)(2,1)}), bf16[8,112,128]{2,1,0:T(8,128)(2,1)S(1)}, u32[]{:S(2)}, u32[]{:S(2)}) %all-to-all-start.2) | async-done | bytes 229408 | tf_op jit(solution)/shard_map/all_to_all | solution.py:701
  73.5 1.2 %collective-permute-done.6 = f32[112,128]{1,0:T(8,128)S(1)} collective-permute-done((f32[112,128]{1,0:T(8,128)S(1)}, f32[112,128]{1,0:T(8,128)S(1)}, u32[]{:S(2)}, u32[]{:S(2)}) %collective-permute-start.6) | collective-permute-done | bytes 57376 | tf_op jit(solution)/shard_map/ppermute | solution.py:705
  74.8 0.7 broadcast_in_dim.2
  75.5 3.9 %all-to-all-start.3 = ((bf16[8,112,128]{2,1,0:T(8,128)(2,1)}), bf16[8,112,128]{2,1,0:T(8,128)(2,1)S(1)}, u32[]{:S(2)}, u32[]{:S(2)}) async-start(bf16[8,112,128]{2,1,0:T(8,128)(2,1)} %broadcast_in_dim.2), calls=%async_computation.3 | async-start | bytes 458752 | tf_op jit(solution)/shard_map/all_to_all | solution.py:708
  79.5 7.0 %input_gradient.3 = bf16[64,2,64,256]{3,2,1,0:T(8,128)(2,1)} custom-call(bf16[8448,384]{1,0:T(8,128)(2,1)} %get-tuple-element.54.masked_hbm, bf16[256,1536]{1,0:T(8,128)(2,1)S(1)} %copy-done.1, bf16[64,2,64,256]{3,2,1,0:T(8,128)(2,1)} %input_gradient.2.rest_0_), custom_call_target="tpu_custom_call", output_to_operand_aliasing={{}: (2, {})} | custom-call | flops 3221225472 | bytes 8388608 | tf_op jit(solution)/shard_map/input_gradient/pallas_call | solution.py:573
  86.4 1.8 %all-to-all-done.3 = bf16[8,112,128]{2,1,0:T(8,128)(2,1)S(1)} async-done(((bf16[8,112,128]{2,1,0:T(8,128)(2,1)}), bf16[8,112,128]{2,1,0:T(8,128)(2,1)S(1)}, u32[]{:S(2)}, u32[]{:S(2)}) %all-to-all-start.3) | async-done | bytes 229408 | tf_op jit(solution)/shard_map/all_to_all | solution.py:708
  88.2 1.0 %unpack.1 = (f32[27,64,64]{2,1,0:T(8,128)}, f32[27,64]{1,0:T(8,128)}) custom-call(bf16[896,128]{1,0:T(8,128)(2,1)S(1)} %bitcast.15), custom_call_target="tpu_custom_call" | custom-call | tf_op jit(solution)/shard_map/unpack/pallas_call | solution.py:610
  (23 shorter events, 0.7 us)
Async XLA Ops:
  0.6 33.1 %copy-start = (bf16[27,64]{1,0:T(8,128)(2,1)S(1)}, bf16[27,64]{1,0:T(8,128)(2,1)}, u32[]{:S(2)}) copy-start(bf16[27,64]{1,0:T(8,128)(2,1)} %param.18) | copy-start | bytes 10372
  1.6 1.5 %collective-permute-start = (f32[2,64,256]{2,1,0:T(8,128)S(1)}, f32[2,64,256]{2,1,0:T(8,128)S(1)}, u32[]{:S(2)}, u32[]{:S(2)}) collective-permute-start(f32[2,64,256]{2,1,0:T(8,128)S(1)} %sub.3.own_ref), channel_id=1, source_target_pairs={{0,1},{1,0},{2,3},{3,2},{4,5},{5,4},{6,7},{7,6},{8,9},{9,8},{10,11... | collective-permute-start | bytes 393224 | tf_op jit(solution)/shard_map/ppermute | solution.py:656
  3.1 10.3 %collective-permute-start.1 = (bf16[64,2,64,256]{3,2,1,0:T(8,128)(2,1)}, bf16[64,2,64,256]{3,2,1,0:T(8,128)(2,1)}, u32[]{:S(2)}, u32[]{:S(2)}) collective-permute-start(bf16[64,2,64,256]{3,2,1,0:T(8,128)(2,1)} %whole), channel_id=1, source_target_pairs={{0,1},{1,0},{2,3},{3,2},{4,5},{5,4},{6,7},{7,6},{8,9},{9,8},{10,11... | collective-permute-start | bytes 12582920 | tf_op jit(solution)/shard_map/ppermute | solution.py:658
  3.5 35.7 %collective-permute-start.5 = (bf16[64,2,64,256]{3,2,1,0:T(8,128)(2,1)}, bf16[64,2,64,256]{3,2,1,0:T(8,128)(2,1)}, u32[]{:S(2)}, u32[]{:S(2)}) collective-permute-start(bf16[64,2,64,256]{3,2,1,0:T(8,128)(2,1)} %in_hbm), channel_id=1, source_target_pairs={{0,1},{1,0},{2,3},{3,2},{4,5},{5,4},{6,7},{7,6},{8,9},{9,8},{10,11... | collective-permute-start | bytes 12582920 | tf_op jit(solution)/shard_map/ppermute | solution.py:659
  6.3 16.5 %all-to-all-start = ((f32[8,64,128]{2,1,0:T(8,128)}), f32[8,64,128]{2,1,0:T(8,128)S(1)}, u32[]{:S(2)}, u32[]{:S(2)}) async-start(f32[8,64,128]{2,1,0:T(8,128)} %forward_y.1), calls=%async_computation | async-start | bytes 524288 | tf_op jit(solution)/shard_map/all_to_all | solution.py:663
  13.4 9.4 %copy-start.4 = (f32[32,512]{1,0:T(8,128)S(1)}, f32[32,512]{1,0:T(8,128)}, u32[]{:S(2)}) copy-start(f32[32,512]{1,0:T(8,128)} %param.14) | copy-start | bytes 196612
  13.4 9.5 %copy-start.2 = (bf16[2,1024,512]{2,1,0:T(8,128)(2,1)S(1)}, bf16[2,1024,512]{2,1,0:T(8,128)(2,1)}, u32[]{:S(2)}) copy-start(bf16[2,1024,512]{2,1,0:T(8,128)(2,1)} %constant.18.clone.table_ref) | copy-start | bytes 6291460
  18.7 15.1 %copy-start.3 = (bf16[27,10,2,128]{3,0,2,1:T(8,128)(2,1)S(1)}, bf16[27,10,2,128]{3,0,2,1:T(8,128)(2,1)}, u32[]{:S(2)}) copy-start(bf16[27,10,2,128]{3,0,2,1:T(8,128)(2,1)} %constant.19.clone) | copy-start | bytes 414724
  18.7 7.5 %collective-permute-start.2 = (bf16[2,128,256]{2,1,0:T(8,128)(2,1)S(1)}, bf16[2,128,256]{2,1,0:T(8,128)(2,1)S(1)}, u32[]{:S(2)}, u32[]{:S(2)}) collective-permute-start(bf16[2,128,256]{2,1,0:T(8,128)(2,1)S(1)} %get-tuple-element.41), channel_id=1, source_target_pairs={{0,2},{2,4},{4,6},{6,8},{8,10},{10,12},{12,14},{3,1},{5,3},{7,5},{... | collective-permute-start | bytes 393224 | tf_op jit(solution)/shard_map/ppermute | solution.py:666
  26.1 13.0 %all-to-all-start.1 = ((bf16[8,72,128]{2,1,0:T(8,128)(2,1)}), bf16[8,72,128]{2,1,0:T(8,128)(2,1)S(1)}, u32[]{:S(2)}, u32[]{:S(2)}) async-start(bf16[8,72,128]{2,1,0:T(8,128)(2,1)} %along_x.1), calls=%async_computation.1 | async-start | bytes 294912 | tf_op jit(solution)/shard_map/all_to_all | solution.py:672
  31.7 2.3 %collective-permute-start.3 = (bf16[2,128,256]{2,1,0:T(8,128)(2,1)S(1)}, bf16[2,128,256]{2,1,0:T(8,128)(2,1)S(1)}, u32[]{:S(2)}, u32[]{:S(2)}) collective-permute-start(bf16[2,128,256]{2,1,0:T(8,128)(2,1)S(1)} %collective-permute-done.2.beyond_ref), channel_id=1, source_target_pairs={{0,1},{1,0},{2,3},{3,2},{4,5},{5,4},{6,7},{7,6},{8,9},{9,8},{10,11... | collective-permute-start | bytes 393224 | tf_op jit(solution)/shard_map/ppermute | solution.py:673
  39.2 1.4 %collective-permute-start.4 = (bf16[8,72,128]{2,1,0:T(8,128)(2,1)S(1)}, bf16[8,72,128]{2,1,0:T(8,128)(2,1)S(1)}, u32[]{:S(2)}, u32[]{:S(2)}) collective-permute-start(bf16[8,72,128]{2,1,0:T(8,128)(2,1)S(1)} %all-to-all-done.1.own_ref), channel_id=1, source_target_pairs={{0,1},{1,0},{2,3},{3,2},{4,5},{5,4},{6,7},{7,6},{8,9},{9,8},{10,11... | collective-permute-start | bytes 442376 | tf_op jit(solution)/shard_map/ppermute | solution.py:682
  40.5 23.9 %copy-start.1 = (bf16[256,1536]{1,0:T(8,128)(2,1)S(1)}, bf16[256,1536]{1,0:T(8,128)(2,1)}, u32[]{:S(2)}) copy-start(bf16[256,1536]{1,0:T(8,128)(2,1)} %arrange.1.weight_ref) | copy-start | bytes 2359300
  61.0 12.4 %all-to-all-start.2 = ((bf16[8,112,128]{2,1,0:T(8,128)(2,1)}), bf16[8,112,128]{2,1,0:T(8,128)(2,1)S(1)}, u32[]{:S(2)}, u32[]{:S(2)}) async-start(bf16[8,112,128]{2,1,0:T(8,128)(2,1)} %bitcast.7), calls=%async_computation.2 | async-start | bytes 458752 | tf_op jit(solution)/shard_map/all_to_all | solution.py:701
  73.5 1.3 %collective-permute-start.6 = (f32[112,128]{1,0:T(8,128)S(1)}, f32[112,128]{1,0:T(8,128)S(1)}, u32[]{:S(2)}, u32[]{:S(2)}) collective-permute-start(f32[112,128]{1,0:T(8,128)S(1)} %convert_reduce_fusion), channel_id=1, source_target_pairs={{0,1},{1,0},{2,3},{3,2},{4,5},{5,4},{6,7},{7,6},{8,9},{9,8},{10,11... | collective-permute-start | bytes 172040 | tf_op jit(solution)/shard_map/ppermute | solution.py:705
  75.5 12.7 %all-to-all-start.3 = ((bf16[8,112,128]{2,1,0:T(8,128)(2,1)}), bf16[8,112,128]{2,1,0:T(8,128)(2,1)S(1)}, u32[]{:S(2)}, u32[]{:S(2)}) async-start(bf16[8,112,128]{2,1,0:T(8,128)(2,1)} %broadcast_in_dim.2), calls=%async_computation.3 | async-start | bytes 458752 | tf_op jit(solution)/shard_map/all_to_all | solution.py:708

commit v3 on v2

--- a/solution.py
+++ b/solution.py
@@ -41,7 +41,7 @@
     shape = (half + 128, wide, 2, keep)
     both = np.stack([cos.reshape(shape), sin.reshape(shape)], axis=2)
     table = split_table(both.reshape(half + 128, wide * 4 * keep))
-    return table[:, :half], table[:, half:]
+    return table[:, :half], table.transpose(0, 2, 1).copy()
 
 
 def x_table(total):
@@ -231,7 +231,6 @@
     own_ref,
     other_ref,
     table_ref,
-    table_side_ref,
     taps_ref,
     beyond_ref,
     beside_ref,
@@ -289,13 +288,7 @@
         [jnp.concatenate(z_lines[0], axis=1), jnp.concatenate(z_lines[1], axis=1)], axis=0
     )
     lines = lines.astype(bf16)
-    noise = jnp.concatenate(
-        [
-            dot_nt(lines, table[0]) + dot_nt(lines, table[1])
-            for table in (table_ref, table_side_ref)
-        ],
-        axis=1,
-    )
+    noise = dot(lines, table_ref[0]) + dot(lines, table_ref[1])
     column = lanes_of((1, ext))
     beside = jnp.where(narrow == 0, column - half, ext - 1 - column) < 2
     ours = (column < half) | beside
@@ -423,7 +416,6 @@
     own,
     other,
     table,
-    table_side,
     taps,
     pick,
     beyond,
@@ -443,7 +435,7 @@
             pltpu.HBM(((rows + 2) * 128, ext), bf16),
             jax.ShapeDtypeStruct((14 * 64, 128), bf16),
         ),
-        in_specs=[pl.BlockSpec(memory_space=pltpu.SMEM)] + [vmem] * 7 + [anywhere] * 4,
+        in_specs=[pl.BlockSpec(memory_space=pltpu.SMEM)] + [vmem] * 6 + [anywhere] * 4,
         out_specs=(anywhere, vmem),
         scratch_shapes=[
             pltpu.VMEM((14 * 64, 128), f32),
@@ -469,7 +461,6 @@
         own,
         other,
         off_chip(table),
-        off_chip(table_side),
         taps,
         beyond,
         beyond_other,
@@ -646,7 +637,7 @@
     swap = [(0, 1), (1, 0)]
     up = [(i, i + 1) for i in range(wide - 1)]
     down = [(j, i) for i, j in up]
-    table_y, table_side = (jnp.asarray(t) for t in y_table(wide, keep, half))
+    table_y, table_back = (jnp.asarray(t) for t in y_table(wide, keep, half))
     table_x = jnp.asarray(x_table(total_x))
     choice = tap_choice()
     pick = np.zeros((16 * 128, 128), np.float32)
@@ -684,8 +675,7 @@
         index,
         lines,
         lines_other,
-        table_y,
-        table_side,
+        table_back,
         taps,
         jnp.asarray(pick, bf16),
         beyond,

time: 89.9 us -> 90.2 us (level)
  no operation moved by 1% of the time
where the time goes in v3:
time: 90.2 us; the launch traced here: 89.5 us
  Pallas kernels  47.7 us (53%)
  starting transfers between devices  25.2 us (28%)
  waiting for transfers between devices  13.5 us (15%)
  other arithmetic  1.03 us (1%)
    pallas_call x1, Pallas kernels, masked_and_kernels(): pl.pallas_call(functools.partial(masked_kernel, scale), out_shape=(pltpu....  20.7 us
    pallas_call x2, Pallas kernels, input_gradient(): pl.pallas_call(functools.partial(input_kernel, base), out_shape=jax.Shape...  13.9 us
    all_to_all x2, starting transfers between devices, fast(): lines = lax.all_to_all(lines, 'wide', 0, 0, tiled=True)  12.7 us
    all_to_all x2, starting transfers between devices, fast(): pay = lax.all_to_all(pay, 'wide', 0, 0, tiled=True)  7.36 us
    pallas_call x1, Pallas kernels, turn_mid(): pl.pallas_call(turn_mid_kernel, out_shape=(pltpu.HBM(shape, bf16), jax.Sh...  5.22 us
    all_to_all x2, waiting for transfers between devices, fast(): lines = lax.all_to_all(lines, 'wide', 0, 0, tiled=True)  5.1 us
    ppermute x1, starting transfers between devices, fast(): beyond = lax.ppermute(sent, ('wide', 'narrow'), ways)  4.07 us
    all_to_all x2, waiting for transfers between devices, fast(): pay = lax.all_to_all(pay, 'wide', 0, 0, tiled=True)  3.79 us
  transfers between devices with their start and end apart: 11, of which 7 were waited for; matrix products, arithmetic and copies ran while one was open for 0% of the time, Pallas kernels for 29%

profile of v3, /device:TPU:0, one launch (start us, length us, event | category | flops | bytes accessed | tf_op | source)
XLA Modules:
  0.0 89.5 jit_solution(16387881762141222565)
XLA Ops:
  0.6 1.0 %sub.3.own_ref = f32[2,64,256]{2,1,0:T(8,128)S(1)} subtract(f32[2,64,256]{2,1,0:T(8,128)} %param.12, f32[2,64,256]{2,1,0:T(8,128)} %param.13) | non-fusion elementwise | flops 32768 | bytes 393216 | tf_op jit(solution)/shard_map/sub | solution.py:646
  1.6 0.5 collective-permute-start
  2.2 1.0 %collective-permute-done.other_ref = f32[2,64,256]{2,1,0:T(8,128)S(1)} collective-permute-done((f32[2,64,256]{2,1,0:T(8,128)S(1)}, f32[2,64,256]{2,1,0:T(8,128)S(1)}, u32[]{:S(2)}, u32[]{:S(2)}) %collective-permute-start) | collective-permute-done | bytes 131104 | tf_op jit(solution)/shard_map/ppermute | solution.py:647
  3.1 0.4 collective-permute-start.1
  3.7 2.6 %forward_y.1 = f32[8,64,128]{2,1,0:T(8,128)} custom-call(s32[1]{0:T(128)} %bitcast.index_ref, f32[2,64,256]{2,1,0:T(8,128)S(1)} %sub.3.own_ref, f32[2,64,256]{2,1,0:T(8,128)S(1)} %collective-permute-done.other_ref, bf16[2,256,1024]{2,1,0:T(8,128)(2,1)} %constant.16.clone.table_ref), custom_call_target="tpu_custom_call" | custom-call | tf_op jit(solution)/shard_map/forward_y/pallas_call | solution.py:108
  6.3 7.2 %all-to-all-start = ((f32[8,64,128]{2,1,0:T(8,128)}), f32[8,64,128]{2,1,0:T(8,128)S(1)}, u32[]{:S(2)}, u32[]{:S(2)}) async-start(f32[8,64,128]{2,1,0:T(8,128)} %forward_y.1), calls=%async_computation | async-start | bytes 524288 | tf_op jit(solution)/shard_map/all_to_all | solution.py:654
  13.5 5.2 %turn_mid.1 = (bf16[64,2,64,384]{3,2,1,0:T(8,128)(2,1)}, bf16[2,128,256]{2,1,0:T(8,128)(2,1)S(1)}) custom-call(s32[1]{0:T(128)} %bitcast.index_ref, bf16[64,2,64,256]{3,2,1,0:T(8,128)(2,1)} %whole, bf16[64,2,64,256]{3,2,1,0:T(8,128)(2,1)} %collective-permute-done.1.other), custom_call_target="tpu_custom_call" | custom-call | bytes 25165824 | tf_op jit(solution)/shard_map/turn_mid/pallas_call | solution.py:208
  18.7 4.1 %collective-permute-start.2 = (bf16[2,128,256]{2,1,0:T(8,128)(2,1)S(1)}, bf16[2,128,256]{2,1,0:T(8,128)(2,1)S(1)}, u32[]{:S(2)}, u32[]{:S(2)}) collective-permute-start(bf16[2,128,256]{2,1,0:T(8,128)(2,1)S(1)} %get-tuple-element.41), channel_id=1, source_target_pairs={{0,2},{2,4},{4,6},{6,8},{8,10},{10,12},{12,14},{3,1},{5,3},{7,5},{... | collective-permute-start | bytes 393224 | tf_op jit(solution)/shard_map/ppermute | solution.py:657
  23.0 2.2 %along_x.1 = bf16[8,72,128]{2,1,0:T(8,128)(2,1)} custom-call(f32[8,64,128]{2,1,0:T(8,128)S(1)} %all-to-all-done.in_ref, bf16[2,1024,512]{2,1,0:T(8,128)(2,1)S(1)} %copy-done.2, f32[512,128]{1,0:T(8,128)S(1)} %copy.17.weight_ref), custom_call_target="tpu_custom_call" | custom-call | tf_op jit(solution)/shard_map/along_x/pallas_call | solution.py:144
  25.1 1.0 %collective-permute-done.2.beyond_ref = bf16[2,128,256]{2,1,0:T(8,128)(2,1)S(1)} collective-permute-done((bf16[2,128,256]{2,1,0:T(8,128)(2,1)S(1)}, bf16[2,128,256]{2,1,0:T(8,128)(2,1)S(1)}, u32[]{:S(2)}, u32[]{:S(2)}) %collective-permute-start.2) | collective-permute-done | bytes 131104 | tf_op jit(solution)/shard_map/ppermute | solution.py:657
  26.1 5.6 %all-to-all-start.1 = ((bf16[8,72,128]{2,1,0:T(8,128)(2,1)}), bf16[8,72,128]{2,1,0:T(8,128)(2,1)S(1)}, u32[]{:S(2)}, u32[]{:S(2)}) async-start(bf16[8,72,128]{2,1,0:T(8,128)(2,1)} %along_x.1), calls=%async_computation.1 | async-start | bytes 294912 | tf_op jit(solution)/shard_map/all_to_all | solution.py:663
  31.7 2.0 %arrange.1.weight_ref = bf16[256,1536]{1,0:T(8,128)(2,1)} custom-call(bf16[27,64,64]{2,1,0:T(8,128)(2,1)} %taps_ref), custom_call_target="tpu_custom_call" | custom-call | tf_op jit(solution)/shard_map/arrange/pallas_call | solution.py:493
  34.1 5.1 %all-to-all-done.1.own_ref = bf16[8,72,128]{2,1,0:T(8,128)(2,1)S(1)} async-done(((bf16[8,72,128]{2,1,0:T(8,128)(2,1)}), bf16[8,72,128]{2,1,0:T(8,128)(2,1)S(1)}, u32[]{:S(2)}, u32[]{:S(2)}) %all-to-all-start.1) | async-done | bytes 147488 | tf_op jit(solution)/shard_map/all_to_all | solution.py:663
  39.2 1.4 %collective-permute-done.4.other_ref = bf16[8,72,128]{2,1,0:T(8,128)(2,1)S(1)} collective-permute-done((bf16[8,72,128]{2,1,0:T(8,128)(2,1)S(1)}, bf16[8,72,128]{2,1,0:T(8,128)(2,1)S(1)}, u32[]{:S(2)}, u32[]{:S(2)}) %collective-permute-start.4) | collective-permute-done | bytes 147488 | tf_op jit(solution)/shard_map/ppermute | solution.py:673
  40.5 20.7 %masked_and_kernels.1 = (bf16[8448,384]{1,0:T(8,128)(2,1)}, bf16[896,128]{1,0:T(8,128)(2,1)}) custom-call(s32[1]{0:T(128)} %bitcast.index_ref, bf16[8,72,128]{2,1,0:T(8,128)(2,1)S(1)} %all-to-all-done.1.own_ref, bf16[8,72,128]{2,1,0:T(8,128)(2,1)S(1)} %collective-permute-done.4.other_ref, bf16[2,1024,384]{2,1,0:T(8,128)(2,1)} %constant.17.clone.table_ref, ...), custom_call_target="tpu_custom_call" | custom-call | tf_op jit(solution)/shard_map/masked_and_kernels/pallas_call | solution.py:432
  61.3 3.4 %all-to-all-start.2 = ((bf16[8,112,128]{2,1,0:T(8,128)(2,1)}), bf16[8,112,128]{2,1,0:T(8,128)(2,1)S(1)}, u32[]{:S(2)}, u32[]{:S(2)}) async-start(bf16[8,112,128]{2,1,0:T(8,128)(2,1)} %bitcast.7), calls=%async_computation.2 | async-start | bytes 458752 | tf_op jit(solution)/shard_map/all_to_all | solution.py:691
  64.7 7.0 %input_gradient.2.rest_0_ = bf16[64,2,64,256]{3,2,1,0:T(8,128)(2,1)} custom-call(bf16[8448,384]{1,0:T(8,128)(2,1)} %get-tuple-element.54.masked_hbm, bf16[256,1536]{1,0:T(8,128)(2,1)S(1)} %copy-done.1), custom_call_target="tpu_custom_call" | custom-call | flops 3221225472 | bytes 8388608 | tf_op jit(solution)/shard_map/input_gradient/pallas_call | solution.py:564
  71.7 2.0 %all-to-all-done.2 = bf16[8,112,128]{2,1,0:T(8,128)(2,1)S(1)} async-done(((bf16[8,112,128]{2,1,0:T(8,128)(2,1)}), bf16[8,112,128]{2,1,0:T(8,128)(2,1)S(1)}, u32[]{:S(2)}, u32[]{:S(2)}) %all-to-all-start.2) | async-done | bytes 229408 | tf_op jit(solution)/shard_map/all_to_all | solution.py:691
  73.8 1.2 %collective-permute-done.6 = f32[112,128]{1,0:T(8,128)S(1)} collective-permute-done((f32[112,128]{1,0:T(8,128)S(1)}, f32[112,128]{1,0:T(8,128)S(1)}, u32[]{:S(2)}, u32[]{:S(2)}) %collective-permute-start.6) | collective-permute-done | bytes 57376 | tf_op jit(solution)/shard_map/ppermute | solution.py:695
  75.0 0.7 broadcast_in_dim.2
  75.7 3.9 %all-to-all-start.3 = ((bf16[8,112,128]{2,1,0:T(8,128)(2,1)}), bf16[8,112,128]{2,1,0:T(8,128)(2,1)S(1)}, u32[]{:S(2)}, u32[]{:S(2)}) async-start(bf16[8,112,128]{2,1,0:T(8,128)(2,1)} %broadcast_in_dim.2), calls=%async_computation.3 | async-start | bytes 458752 | tf_op jit(solution)/shard_map/all_to_all | solution.py:698
  79.7 7.0 %input_gradient.3 = bf16[64,2,64,256]{3,2,1,0:T(8,128)(2,1)} custom-call(bf16[8448,384]{1,0:T(8,128)(2,1)} %get-tuple-element.54.masked_hbm, bf16[256,1536]{1,0:T(8,128)(2,1)S(1)} %copy-done.1, bf16[64,2,64,256]{3,2,1,0:T(8,128)(2,1)} %input_gradient.2.rest_0_), custom_call_target="tpu_custom_call", output_to_operand_aliasing={{}: (2, {})} | custom-call | flops 3221225472 | bytes 8388608 | tf_op jit(solution)/shard_map/input_gradient/pallas_call | solution.py:564
  86.6 1.8 %all-to-all-done.3 = bf16[8,112,128]{2,1,0:T(8,128)(2,1)S(1)} async-done(((bf16[8,112,128]{2,1,0:T(8,128)(2,1)}), bf16[8,112,128]{2,1,0:T(8,128)(2,1)S(1)}, u32[]{:S(2)}, u32[]{:S(2)}) %all-to-all-start.3) | async-done | bytes 229408 | tf_op jit(solution)/shard_map/all_to_all | solution.py:698
  88.4 1.0 %unpack.1 = (f32[27,64,64]{2,1,0:T(8,128)}, f32[27,64]{1,0:T(8,128)}) custom-call(bf16[896,128]{1,0:T(8,128)(2,1)S(1)} %bitcast.15), custom_call_target="tpu_custom_call" | custom-call | tf_op jit(solution)/shard_map/unpack/pallas_call | solution.py:601
  (23 shorter events, 0.7 us)
Async XLA Ops:
  0.6 33.1 %copy-start = (bf16[27,64]{1,0:T(8,128)(2,1)S(1)}, bf16[27,64]{1,0:T(8,128)(2,1)}, u32[]{:S(2)}) copy-start(bf16[27,64]{1,0:T(8,128)(2,1)} %param.18) | copy-start | bytes 10372
  1.6 1.5 %collective-permute-start = (f32[2,64,256]{2,1,0:T(8,128)S(1)}, f32[2,64,256]{2,1,0:T(8,128)S(1)}, u32[]{:S(2)}, u32[]{:S(2)}) collective-permute-start(f32[2,64,256]{2,1,0:T(8,128)S(1)} %sub.3.own_ref), channel_id=1, source_target_pairs={{0,1},{1,0},{2,3},{3,2},{4,5},{5,4},{6,7},{7,6},{8,9},{9,8},{10,11... | collective-permute-start | bytes 393224 | tf_op jit(solution)/shard_map/ppermute | solution.py:647
  3.1 10.3 %collective-permute-start.1 = (bf16[64,2,64,256]{3,2,1,0:T(8,128)(2,1)}, bf16[64,2,64,256]{3,2,1,0:T(8,128)(2,1)}, u32[]{:S(2)}, u32[]{:S(2)}) collective-permute-start(bf16[64,2,64,256]{3,2,1,0:T(8,128)(2,1)} %whole), channel_id=1, source_target_pairs={{0,1},{1,0},{2,3},{3,2},{4,5},{5,4},{6,7},{7,6},{8,9},{9,8},{10,11... | collective-permute-start | bytes 12582920 | tf_op jit(solution)/shard_map/ppermute | solution.py:649
  3.5 35.7 %collective-permute-start.5 = (bf16[64,2,64,256]{3,2,1,0:T(8,128)(2,1)}, bf16[64,2,64,256]{3,2,1,0:T(8,128)(2,1)}, u32[]{:S(2)}, u32[]{:S(2)}) collective-permute-start(bf16[64,2,64,256]{3,2,1,0:T(8,128)(2,1)} %in_hbm), channel_id=1, source_target_pairs={{0,1},{1,0},{2,3},{3,2},{4,5},{5,4},{6,7},{7,6},{8,9},{9,8},{10,11... | collective-permute-start | bytes 12582920 | tf_op jit(solution)/shard_map/ppermute | solution.py:650
  6.3 16.5 %all-to-all-start = ((f32[8,64,128]{2,1,0:T(8,128)}), f32[8,64,128]{2,1,0:T(8,128)S(1)}, u32[]{:S(2)}, u32[]{:S(2)}) async-start(f32[8,64,128]{2,1,0:T(8,128)} %forward_y.1), calls=%async_computation | async-start | bytes 524288 | tf_op jit(solution)/shard_map/all_to_all | solution.py:654
  13.4 9.4 %copy-start.4 = (f32[32,512]{1,0:T(8,128)S(1)}, f32[32,512]{1,0:T(8,128)}, u32[]{:S(2)}) copy-start(f32[32,512]{1,0:T(8,128)} %param.14) | copy-start | bytes 196612
  13.4 9.5 %copy-start.2 = (bf16[2,1024,512]{2,1,0:T(8,128)(2,1)S(1)}, bf16[2,1024,512]{2,1,0:T(8,128)(2,1)}, u32[]{:S(2)}) copy-start(bf16[2,1024,512]{2,1,0:T(8,128)(2,1)} %constant.18.clone.table_ref) | copy-start | bytes 6291460
  18.7 15.1 %copy-start.3 = (bf16[27,10,2,128]{3,0,2,1:T(8,128)(2,1)S(1)}, bf16[27,10,2,128]{3,0,2,1:T(8,128)(2,1)}, u32[]{:S(2)}) copy-start(bf16[27,10,2,128]{3,0,2,1:T(8,128)(2,1)} %constant.19.clone) | copy-start | bytes 414724
  18.7 7.5 %collective-permute-start.2 = (bf16[2,128,256]{2,1,0:T(8,128)(2,1)S(1)}, bf16[2,128,256]{2,1,0:T(8,128)(2,1)S(1)}, u32[]{:S(2)}, u32[]{:S(2)}) collective-permute-start(bf16[2,128,256]{2,1,0:T(8,128)(2,1)S(1)} %get-tuple-element.41), channel_id=1, source_target_pairs={{0,2},{2,4},{4,6},{6,8},{8,10},{10,12},{12,14},{3,1},{5,3},{7,5},{... | collective-permute-start | bytes 393224 | tf_op jit(solution)/shard_map/ppermute | solution.py:657
  26.1 13.0 %all-to-all-start.1 = ((bf16[8,72,128]{2,1,0:T(8,128)(2,1)}), bf16[8,72,128]{2,1,0:T(8,128)(2,1)S(1)}, u32[]{:S(2)}, u32[]{:S(2)}) async-start(bf16[8,72,128]{2,1,0:T(8,128)(2,1)} %along_x.1), calls=%async_computation.1 | async-start | bytes 294912 | tf_op jit(solution)/shard_map/all_to_all | solution.py:663
  31.7 2.3 %collective-permute-start.3 = (bf16[2,128,256]{2,1,0:T(8,128)(2,1)S(1)}, bf16[2,128,256]{2,1,0:T(8,128)(2,1)S(1)}, u32[]{:S(2)}, u32[]{:S(2)}) collective-permute-start(bf16[2,128,256]{2,1,0:T(8,128)(2,1)S(1)} %collective-permute-done.2.beyond_ref), channel_id=1, source_target_pairs={{0,1},{1,0},{2,3},{3,2},{4,5},{5,4},{6,7},{7,6},{8,9},{9,8},{10,11... | collective-permute-start | bytes 393224 | tf_op jit(solution)/shard_map/ppermute | solution.py:664
  39.2 1.4 %collective-permute-start.4 = (bf16[8,72,128]{2,1,0:T(8,128)(2,1)S(1)}, bf16[8,72,128]{2,1,0:T(8,128)(2,1)S(1)}, u32[]{:S(2)}, u32[]{:S(2)}) collective-permute-start(bf16[8,72,128]{2,1,0:T(8,128)(2,1)S(1)} %all-to-all-done.1.own_ref), channel_id=1, source_target_pairs={{0,1},{1,0},{2,3},{3,2},{4,5},{5,4},{6,7},{7,6},{8,9},{9,8},{10,11... | collective-permute-start | bytes 442376 | tf_op jit(solution)/shard_map/ppermute | solution.py:673
  40.5 24.2 %copy-start.1 = (bf16[256,1536]{1,0:T(8,128)(2,1)S(1)}, bf16[256,1536]{1,0:T(8,128)(2,1)}, u32[]{:S(2)}) copy-start(bf16[256,1536]{1,0:T(8,128)(2,1)} %arrange.1.weight_ref) | copy-start | bytes 2359300
  61.3 12.4 %all-to-all-start.2 = ((bf16[8,112,128]{2,1,0:T(8,128)(2,1)}), bf16[8,112,128]{2,1,0:T(8,128)(2,1)S(1)}, u32[]{:S(2)}, u32[]{:S(2)}) async-start(bf16[8,112,128]{2,1,0:T(8,128)(2,1)} %bitcast.7), calls=%async_computation.2 | async-start | bytes 458752 | tf_op jit(solution)/shard_map/all_to_all | solution.py:691
  73.7 1.3 %collective-permute-start.6 = (f32[112,128]{1,0:T(8,128)S(1)}, f32[112,128]{1,0:T(8,128)S(1)}, u32[]{:S(2)}, u32[]{:S(2)}) collective-permute-start(f32[112,128]{1,0:T(8,128)S(1)} %convert_reduce_fusion), channel_id=1, source_target_pairs={{0,1},{1,0},{2,3},{3,2},{4,5},{5,4},{6,7},{7,6},{8,9},{9,8},{10,11... | collective-permute-start | bytes 172040 | tf_op jit(solution)/shard_map/ppermute | solution.py:695
  75.7 12.7 %all-to-all-start.3 = ((bf16[8,112,128]{2,1,0:T(8,128)(2,1)}), bf16[8,112,128]{2,1,0:T(8,128)(2,1)S(1)}, u32[]{:S(2)}, u32[]{:S(2)}) async-start(bf16[8,112,128]{2,1,0:T(8,128)(2,1)} %broadcast_in_dim.2), calls=%async_computation.3 | async-start | bytes 458752 | tf_op jit(solution)/shard_map/all_to_all | solution.py:698
